TPU v7x, 32 devices: a whole 2x2x4 slice. The times are simulated.
32 devices in a mesh: dp: 4 (over z), ctx: 4 (over x, core), tp: 2 (over y).
Axes of the slice: x: 2, y: 2, z: 4, core: 2. Of those that a mesh axis runs over, the one named last changes fastest.
Arguments:
- hidden: bfloat16 [12288, 768], P(('dp', 'ctx', 'tp')), may hold values from -6 to 6
- grad_output: bfloat16 [4096, 2048], P(('dp', 'ctx', 'tp')), may hold values from -6 to 6
- expert_ids: int32 [4096, 2], P(('dp', 'ctx', 'tp')), may hold values from 0 to 7, all different within a row; in each aligned block of 128 rows (0 to 127, 128 to 255, ...) at most 48 rows name the same one
- gate_weights: float32 [4096, 2], P(('dp', 'ctx', 'tp')), may hold values from 0.2 to 1
- w_down: bfloat16 [8, 768, 2048], P(('ctx', 'tp')), may hold values from -0.21875 to 0.21875
Outputs:
- combined: bfloat16 [4096, 2048], P(('dp', 'ctx', 'tp'))
- grad_hidden: bfloat16 [12288, 768], P(('dp', 'ctx', 'tp'))
- grad_down: bfloat16 [8, 768, 2048], P(('ctx', 'tp'), 'dp')
Inputs may be any that keep to these rules, and one draw needn't show every extreme that they name: `expert_ids`: each row names 2 different experts. Among the 128 rows of one device no expert is named more than 48 times, and in every draw some device names some expert exactly 48 times.
All inputs are finite; a program needn't handle non-finite values.
Results may differ from a plain program's by a relative error of at most 0.017.
Values may be sent and summed in bfloat16 or wider, within the bound.
No kernel may reach another device: no remote copies, remote signals or barrier semaphores. Data moves between devices by JAX's collectives and lax.ppermute only.
A program may use at most 64 MiB of HBM per device.

v0:
```python
import jax
import jax.numpy as jnp
from jax import lax
from jax.sharding import PartitionSpec as P

grad_scale = 0.015625


def slot_index(ids_block, experts, capacity):
    flat_ids = ids_block.reshape(-1)
    one_hot = (flat_ids[:, None] == jnp.arange(experts, dtype=jnp.int32)[None, :]).astype(jnp.int32)
    earlier = jnp.cumsum(one_hot, axis=0) - one_hot
    ranking = jnp.sum(earlier * one_hot, axis=1)
    return flat_ids * capacity + ranking


def local(hidden, grad_output, expert_ids, gate_weights, w_down):
    ctx_count = lax.axis_size("ctx")
    tp_count = lax.axis_size("tp")
    experts = ctx_count * tp_count
    capacity = hidden.shape[0] // experts
    tok_rows, choices = expert_ids.shape
    model_width = grad_output.shape[1]
    weight = w_down[0]
    positions = slot_index(expert_ids, experts, capacity)
    expert_out = jnp.dot(hidden, weight, preferred_element_type=jnp.float32).astype(jnp.bfloat16)
    expert_out = expert_out.reshape(experts, capacity, model_width)
    returned = lax.all_to_all(expert_out, ("ctx", "tp"), split_axis=0, concat_axis=0, tiled=True)
    returned = returned.reshape(experts * capacity, model_width)
    picked = returned[positions].astype(jnp.float32).reshape(tok_rows, choices, model_width)
    combined = jnp.sum(gate_weights[:, :, None] * picked, axis=1).astype(jnp.bfloat16)
    scaled = (gate_weights[:, :, None] * grad_output[:, None, :].astype(jnp.float32)).astype(
        jnp.bfloat16
    )
    scaled = scaled.reshape(tok_rows * choices, model_width)
    outgoing = jnp.zeros((experts * capacity, model_width), jnp.bfloat16).at[positions].set(scaled)
    outgoing = outgoing.reshape(experts, capacity, model_width)
    incoming = lax.all_to_all(outgoing, ("ctx", "tp"), split_axis=0, concat_axis=0, tiled=True)
    incoming = incoming.reshape(experts * capacity, model_width)
    grad_hidden = lax.dot_general(
        incoming, weight, (((1,), (1,)), ((), ())), preferred_element_type=jnp.float32
    ).astype(jnp.bfloat16)
    summed = lax.psum_scatter(
        lax.dot_general(
            hidden, incoming, (((0,), (0,)), ((), ())), preferred_element_type=jnp.float32
        ).astype(jnp.bfloat16),
        "dp",
        scatter_dimension=0,
        tiled=True,
    ).astype(jnp.float32)
    grad_down = (summed * grad_scale).astype(jnp.bfloat16)[None]
    return (combined, grad_hidden, grad_down)


def solution(mesh):
    return jax.shard_map(
        local,
        mesh=mesh,
        in_specs=(
            P(("dp", "ctx", "tp"), None),
            P(("dp", "ctx", "tp"), None),
            P(("dp", "ctx", "tp"), None),
            P(("dp", "ctx", "tp"), None),
            P(("ctx", "tp"), None, None),
        ),
        out_specs=(
            P(("dp", "ctx", "tp"), None),
            P(("dp", "ctx", "tp"), None),
            P(("ctx", "tp"), "dp", None),
        ),
        check_vma=False,
    )
```

profile of v0, /device:TPU:0, one launch (start us, length us, event | category | flops | bytes accessed | tf_op | source)
XLA Modules:
  0.0 132.2 jit_solution(5789139467107204207)
XLA Ops:
  7.2 0.0 copy-start
  7.2 0.0 reduce-scatter.4.cloned.1.call-start
  7.2 0.8 broadcast_multiply_fusion
  8.1 0.9 copy.18
  8.9 0.1 eq.29
  9.1 0.1 eq.25
  9.2 0.1 copy.17
  9.3 0.1 mul.54
  9.5 0.8 copy.16
  10.2 0.1 mul.57
  10.4 0.6 reduce-window.6
  11.0 0.2 slice_reduce_fusion
  11.2 3.4 %mul.59 = f32[128,2,2048]{2,1,0:T(2,128)} broadcast(bf16[128,2048]{1,0:T(8,128)(2,1)} %param.6), dimensions={0,2} | broadcast | bytes 2621440 | tf_op jit(solution)/shard_map/mul | solution.py:32
  14.6 3.7 %mul.60 = f32[256,2048]{1,0:T(8,128)} reshape(f32[128,2,2048]{2,1,0:T(2,128)} %mul.59) | data formatting | bytes 4194304 | tf_op jit(solution)/shard_map/mul | solution.py:32
  18.3 0.1 fusion.16
  18.4 4.5 %scatter_custom_fusion = bf16[384,2048]{1,0:T(8,128)(2,1)} fusion(s32[256]{0:T(256)S(1)} %bitcast.37, f32[256,2048]{1,0:T(8,128)} %mul.60, f32[256]{0:T(256)S(1)} %mul.57, bf16[]{:T(256)} %constant.5.clone.1), kind=kCustom, calls=%fused_computation.13 | custom fusion | flops 1048576 | bytes 3671042 | tf_op jit(solution)/shard_map/scatter | solution.py:36
  23.0 0.0 copy-start.3
  23.0 25.4 %all_to_all.10 = bf16[8,48,2048]{2,1,0:T(8,128)(2,1)S(1)} all-to-all(bf16[8,48,2048]{2,1,0:T(8,128)(2,1)} %bitcast.33), channel_id=1, replica_groups=mesh['dp'=4,'ctx'=4,'tp'=2] {'ctx','tp'}, dimensions={0} | all-to-all | bytes 3145728 | tf_op jit(solution)/shard_map/all_to_all | solution.py:38
  48.4 0.0 copy-start.1
  48.4 1.1 copy-done.1
  49.5 0.0 copy-done.3
  49.5 3.5 %fusion.4 = bf16[768,2048]{0,1:T(8,128)(2,1)} fusion(bf16[384,2048]{1,0:T(8,128)(2,1)S(1)} %bitcast.34, bf16[384,768]{1,0:T(8,128)(2,1)S(1)} %copy-done.3), kind=kOutput, calls=%fused_computation.7 | convolution fusion | flops 1209532416 | bytes 5308416 | tf_op jit(solution)/shard_map/dot_general | solution.py:44
  53.1 4.8 %copy.22 = bf16[768,2048]{1,0:T(8,128)(2,1)} copy(bf16[768,2048]{0,1:T(8,128)(2,1)} %fusion.4) | data formatting | bytes 6291456
  57.8 0.0 reduce-scatter.4.cloned.1.call-update
  57.8 0.0 copy-done
  57.9 3.6 %fusion.5 = bf16[384,2048]{1,0:T(8,128)(2,1)} fusion(bf16[384,768]{1,0:T(8,128)(2,1)} %param.5, bf16[1,768,2048]{2,1,0:T(8,128)(2,1)S(1)} %copy-done), kind=kOutput, calls=%fused_computation.8 | convolution fusion | flops 1208745984 | bytes 5308416 | tf_op jit(solution)/shard_map/dot_general | solution.py:26
  61.5 4.6 %all-to-all-start = ((bf16[8,48,2048]{2,1,0:T(8,128)(2,1)}), bf16[8,48,2048]{2,1,0:T(8,128)(2,1)}, u32[]{:S(2)}, u32[]{:S(2)}) async-start(bf16[8,48,2048]{2,1,0:T(8,128)(2,1)} %bitcast.36), calls=%async_computation | async-start | bytes 3145728 | tf_op jit(solution)/shard_map/all_to_all | solution.py:28
  66.1 20.0 %all-to-all-done = bf16[8,48,2048]{2,1,0:T(8,128)(2,1)} async-done(((bf16[8,48,2048]{2,1,0:T(8,128)(2,1)}), bf16[8,48,2048]{2,1,0:T(8,128)(2,1)}, u32[]{:S(2)}, u32[]{:S(2)}) %all-to-all-start) | async-done | bytes 1572896 | tf_op jit(solution)/shard_map/all_to_all | solution.py:28
  86.0 5.0 %gather_fusion = bf16[256,2048]{1,0:T(8,128)(2,1)} fusion(bf16[384,2048]{1,0:T(8,128)(2,1)} %bitcast.2, s32[1024]{0:T(1024)S(1)} %pad_clamp_fusion), kind=kCustom, calls=%fused_computation | custom fusion | bytes 2098176 | tf_op jit(solution)/shard_map/gather | solution.py:30
  91.0 3.3 %reshape.79 = f32[128,2,2048]{2,1,0:T(2,128)} reshape(bf16[256,2048]{1,0:T(8,128)(2,1)} %gather_fusion) | data formatting | bytes 3145728 | tf_op jit(solution)/shard_map/convert_element_type | solution.py:30
  94.4 0.0 copy-start.2
  94.4 5.7 %multiply_reduce_fusion = bf16[128,2048]{1,0:T(8,128)(2,1)} fusion(f32[128,2,2048]{2,1,0:T(2,128)} %reshape.79, f32[128,2]{1,0:T(8,128)S(1)} %copy.16), kind=kLoop, calls=%fused_computation.11 | loop fusion | flops 786432 | bytes 2622464 | tf_op jit(solution)/shard_map/reduce_sum | solution.py:31
  100.1 0.0 copy-done.2
  100.1 2.2 %fusion.8 = bf16[384,768]{1,0:T(8,128)(2,1)} fusion(bf16[384,2048]{1,0:T(8,128)(2,1)S(1)} %bitcast.35, bf16[1,768,2048]{2,1,0:T(8,128)(2,1)S(1)} %copy-done), kind=kOutput, calls=%fused_computation.12 | convolution fusion | flops 1208254464 | bytes 5308416 | tf_op jit(solution)/shard_map/dot_general | solution.py:40
  102.3 16.2 %reduce-scatter.4.cloned.1.call-done = bf16[192,2048]{1,0:T(8,128)(2,1)} async-done(((bf16[768,2048]{1,0:T(8,128)(2,1)}), bf16[192,2048]{1,0:T(8,128)(2,1)}) %reduce-scatter.4.cloned.1.call-update) | async-done | bytes 786448
  118.5 2.2 %copy.23 = bf16[192,2048]{0,1:T(8,128)(2,1)} copy(bf16[192,2048]{1,0:T(8,128)(2,1)} %reduce-scatter.4.cloned.1.call-done) | data formatting | bytes 1572864
  120.8 2.4 %fusion.12 = bf16[1,192,2048]{1,2,0:T(8,128)(2,1)} fusion(bf16[192,2048]{0,1:T(8,128)(2,1)} %copy.23), kind=kLoop, calls=%fused_computation.14 | loop fusion | flops 1179648 | bytes 1572864 | tf_op jit(solution)/shard_map/broadcast_in_dim | solution.py:51
  123.2 2.2 %copy.21 = bf16[1,192,2048]{2,1,0:T(8,128)(2,1)} copy(bf16[1,192,2048]{1,2,0:T(8,128)(2,1)} %fusion.12) | data formatting | bytes 1572864
  (5 shorter events, 0.1 us)
Async XLA Ops:
  7.2 50.7 %copy-start = (bf16[1,768,2048]{2,1,0:T(8,128)(2,1)S(1)}, bf16[1,768,2048]{2,1,0:T(8,128)(2,1)}, u32[]{:S(2)}) copy-start(bf16[1,768,2048]{2,1,0:T(8,128)(2,1)} %param.9) | copy-start | bytes 9437188
  7.2 111.4 %reduce-scatter.4.cloned.1.call-start = ((), (), s32[]{:S(2)}) async-start(), calls=%async_computation.3 | async-start | bytes 3932160
  23.0 26.5 %copy-start.3 = (bf16[384,768]{1,0:T(8,128)(2,1)S(1)}, bf16[384,768]{1,0:T(8,128)(2,1)}, u32[]{:S(2)}) copy-start(bf16[384,768]{1,0:T(8,128)(2,1)} %param.5) | copy-start | bytes 1769476
  48.4 1.1 copy-start.1
  61.5 24.6 %all-to-all-start = ((bf16[8,48,2048]{2,1,0:T(8,128)(2,1)}), bf16[8,48,2048]{2,1,0:T(8,128)(2,1)}, u32[]{:S(2)}, u32[]{:S(2)}) async-start(bf16[8,48,2048]{2,1,0:T(8,128)(2,1)} %bitcast.36), calls=%async_computation | async-start | bytes 3145728 | tf_op jit(solution)/shard_map/all_to_all | solution.py:28
  94.4 5.7 %copy-start.2 = (bf16[8,48,2048]{2,1,0:T(8,128)(2,1)S(1)}, bf16[8,48,2048]{2,1,0:T(8,128)(2,1)}, u32[]{:S(2)}) copy-start(bf16[8,48,2048]{2,1,0:T(8,128)(2,1)} %copy-done.1) | copy-start | bytes 4718596
Sparse Core Ops, SparseCore 0:
  58.0 60.5 reduce-scatter.3
where the time goes:
time: 133 us; the launch traced here: 132 us
  waiting for transfers between devices  36.2 us (27%)
  local copies, waits for them, and re-layouts  28.3 us (21%)
  blocking collectives  25.4 us (19%)
  other arithmetic  14.2 us (11%)
  between operations  14.1 us (11%)
  matrix products  9.41 us (7%)
  starting transfers between devices  4.6 us (3%)
    all_to_all x1, blocking collectives, local(): lax.all_to_all(outgoing, ('ctx', 'tp'), split_axis=0, concat_axis=0, tile...  25.4 us
    all_to_all x1, waiting for transfers between devices, local(): lax.all_to_all(expert_out, ('ctx', 'tp'), split_axis=0, concat_axis=0, ti...  20 us
    unnamed x2, waiting for transfers between devices  16.2 us
    unnamed x13, local copies, waits for them, and re-layouts  12 us
    mul x2, local copies, waits for them, and re-layouts, local(): gate_weights[:, :, None] * grad_output[:, None, :].astype(jnp.float32)  7.11 us
    reduce_sum x1, other arithmetic, local(): jnp.sum(gate_weights[:, :, None] * picked, axis=1).astype(jnp.bfloat16)  5.71 us
    gather x1, local copies, waits for them, and re-layouts, local(): returned[positions].astype(jnp.float32)  5.01 us
    all_to_all x1, starting transfers between devices, local(): lax.all_to_all(expert_out, ('ctx', 'tp'), split_axis=0, concat_axis=0, ti...  4.56 us
  transfers between devices with their start and end apart: 2, of which 2 were waited for; matrix products, arithmetic and copies ran while one was open for 15% of the time, Pallas kernels for 0%

commit v1 on v0

v1 whole, which is shorter than its diff:
```python
import jax
import jax.numpy as jnp
from jax import lax
from jax.experimental import pallas as pl
from jax.experimental.pallas import tpu as pltpu
from jax.sharding import PartitionSpec as P

grad_scale = 0.015625
PIECES = 4
F32 = jnp.float32
BF16 = jnp.bfloat16


def call(body, outs, ins, name, flops=0, smem=0):
    moved = sum(a.size * a.dtype.itemsize for a in (*ins, *outs))
    in_specs = [
        pl.BlockSpec(memory_space=pltpu.SMEM if i < smem else pltpu.VMEM) for i in range(len(ins))
    ]
    return pl.pallas_call(
        body,
        out_shape=tuple(outs),
        in_specs=in_specs,
        out_specs=tuple(pl.BlockSpec(memory_space=pltpu.VMEM) for _ in outs),
        name=name,
        cost_estimate=pl.CostEstimate(flops=flops, bytes_accessed=moved, transcendentals=0),
        compiler_params=pltpu.CompilerParams(vmem_limit_bytes=24 * 2**20),
    )(*ins)


def iota(shape, axis):
    return lax.broadcasted_iota(jnp.int32, shape, axis)


def slot_rows(ids, experts, capacity):
    choices, tokens = ids.shape
    named = [(iota((experts, tokens), 0) == ids[k : k + 1]).astype(F32) for k in range(choices)]
    before = (iota((tokens, tokens), 0) < iota((tokens, tokens), 1)).astype(BF16)
    earlier = jnp.dot(sum(named).astype(BF16), before, preferred_element_type=F32)
    slots = []
    for k in range(choices):
        rank = jnp.sum(named[k] * earlier, axis=0, keepdims=True)
        slots.append(ids[k : k + 1] * capacity + rank.astype(jnp.int32))
        earlier = earlier + named[k]
    return slots


def dispatch(ids, gates, grads, experts, capacity, widths):
    choices, tokens = ids.shape
    rows = experts * capacity

    def body(ids_ref, gates_ref, grads_ref, *out_refs):
        slots = slot_rows(ids_ref[...], experts, capacity)
        pick = jnp.zeros((rows, tokens), F32)
        scale = jnp.zeros((rows, 1), F32)
        for k in range(choices):
            hit = iota((rows, tokens), 0) == slots[k]
            pick = pick + hit.astype(F32)
            scale = scale + jnp.sum(jnp.where(hit, gates_ref[k : k + 1, :], 0.0), axis=1, keepdims=True)
        pick = pick.astype(BF16)
        start = 0
        for ref, width in zip(out_refs, widths):
            chosen = jnp.dot(pick, grads_ref[:, start : start + width], preferred_element_type=F32)
            ref[...] = (chosen * scale).astype(BF16)
            start += width

    return call(
        body,
        [jax.ShapeDtypeStruct((rows, w), BF16) for w in widths],
        [ids, gates, grads],
        "dispatch",
        2 * rows * tokens * sum(widths),
    )


def combine(ids, gates, returned, experts, capacity):
    choices, tokens = ids.shape
    rows, width = returned.shape

    def body(ids_ref, gates_ref, returned_ref, out_ref):
        slots = slot_rows(ids_ref[...], experts, capacity)
        same = iota((tokens, tokens), 0) == iota((tokens, tokens), 1)
        picks, scales = [], []
        for k in range(choices):
            slot = jnp.sum(jnp.where(same, slots[k], 0), axis=1, keepdims=True)
            picks.append((iota((tokens, rows), 1) == slot).astype(F32).astype(BF16))
            scales.append(jnp.sum(jnp.where(same, gates_ref[k : k + 1, :], 0.0), axis=1, keepdims=True))
        step = min(512, width)
        for start in range(0, width, step):
            block = returned_ref[:, start : start + step]
            out_ref[:, start : start + step] = sum(
                jnp.dot(p, block, preferred_element_type=F32) * s for p, s in zip(picks, scales)
            ).astype(BF16)

    return call(
        body,
        [jax.ShapeDtypeStruct((tokens, width), BF16)],
        [ids, gates, returned],
        "combine",
        2 * choices * rows * tokens * width,
    )[0]


def grad_rows(pieces, weight):
    rows, hidden_units = pieces[0].shape[0], weight.shape[0]

    def body(weight_ref, *refs):
        *piece_refs, out_ref = refs
        total, start = None, 0
        for ref in piece_refs:
            width = ref.shape[1]
            part = lax.dot_general(
                ref[...],
                weight_ref[:, start : start + width],
                (((1,), (1,)), ((), ())),
                preferred_element_type=F32,
            )
            total = part if total is None else total + part
            start += width
        out_ref[...] = total.astype(BF16)

    return call(
        body,
        [jax.ShapeDtypeStruct((rows, hidden_units), BF16)],
        [weight, *pieces],
        "grad_rows",
        2 * rows * weight.size,
    )[0]


def exchange(x, experts):
    shaped = x.reshape(experts, -1, x.shape[1])
    return lax.all_to_all(shaped, ("ctx", "tp"), split_axis=0, concat_axis=0, tiled=True).reshape(x.shape)


def folded_parts(side, mine, theirs, piece, piece_theirs):
    half, width = mine.shape[1] // 2, piece.shape[1]

    def body(side_ref, mine_ref, theirs_ref, piece_ref, piece_theirs_ref, give_ref, keep_ref):
        def rows(which):
            columns = pl.ds(pl.multiple_of(which * half, half), half)
            return sum(
                lax.dot_general(h[:, columns], p[...], (((0,), (0,)), ((), ())), preferred_element_type=F32)
                for h, p in ((mine_ref, piece_ref), (theirs_ref, piece_theirs_ref))
            )

        give_ref[...] = rows(1 - side_ref[0]).astype(BF16)
        keep_ref[...] = rows(side_ref[0])

    return call(
        body,
        [jax.ShapeDtypeStruct((half, width), BF16), jax.ShapeDtypeStruct((half, width), F32)],
        [side, mine, theirs, piece, piece_theirs],
        "folded_parts",
        8 * mine.shape[0] * half * width,
        smem=1,
    )


def finish(side, keep, got):
    half, width = keep.shape
    share = half // 2

    def body(side_ref, keep_ref, got_ref, own_ref, give_ref):
        def rows(which):
            at = pl.ds(pl.multiple_of(which * share, share), share)
            return ((keep_ref[at, :] + got_ref[at, :].astype(F32)) * grad_scale).astype(BF16)

        give_ref[...] = rows(side_ref[0])
        own_ref[...] = rows(1 - side_ref[0])

    return call(
        body,
        [jax.ShapeDtypeStruct((share, width), BF16)] * 2,
        [side, keep, got],
        "finish",
        smem=1,
    )


def local(hidden, grad_output, expert_ids, gate_weights, w_down):
    replicas = lax.axis_size("dp")
    experts = lax.axis_size("ctx") * lax.axis_size("tp")
    capacity = hidden.shape[0] // experts
    width = grad_output.shape[1]
    weight = w_down[0]
    ids, gates = expert_ids.T, gate_weights.T
    widths = [width // PIECES] * PIECES

    outgoing = dispatch(ids, gates, grad_output, experts, capacity, widths)
    pieces = [exchange(x, experts) for x in outgoing]
    if replicas == 4:
        place = lax.axis_index("dp")
        side = (place // 2).reshape(1)
        at_end = (place == 0) | (place == replicas - 1)
        fold, swap, back = [(0, 1), (3, 2)], [(1, 2), (2, 1)], [(1, 0), (2, 3)]
        theirs = lax.ppermute(hidden, "dp", fold)
        shares = []
        for piece in pieces:
            give, keep = folded_parts(side, hidden, theirs, piece, lax.ppermute(piece, "dp", fold))
            own, give = finish(side, keep, lax.ppermute(give, "dp", swap))
            shares.append(jnp.where(at_end, lax.ppermute(give, "dp", back), own))
        grad_down = jnp.concatenate(shares, axis=1)
    else:
        incoming = jnp.concatenate(pieces, axis=1)
        part = lax.dot_general(hidden, incoming, (((0,), (0,)), ((), ())), preferred_element_type=F32)
        summed = lax.psum_scatter(part.astype(BF16), "dp", scatter_dimension=0, tiled=True)
        grad_down = (summed.astype(F32) * grad_scale).astype(BF16)

    expert_out = jnp.dot(hidden, weight, preferred_element_type=F32).astype(BF16)
    returned = exchange(expert_out, experts)
    combined = combine(ids, gates, returned, experts, capacity)
    grad_hidden = grad_rows(pieces, weight)
    return (combined, grad_hidden, grad_down[None])


def solution(mesh):
    rows = P(("dp", "ctx", "tp"), None)
    return jax.shard_map(
        local,
        mesh=mesh,
        in_specs=(rows, rows, rows, rows, P(("ctx", "tp"), None, None)),
        out_specs=(rows, rows, P(("ctx", "tp"), "dp", None)),
        check_vma=False,
    )
```

time: 133 us -> 122 us (0.917)
  starting transfers between devices: 4.6 us -> 34.1 us
  local copies, waits for them, and re-layouts: 28.3 us -> 6.1 us
  Pallas kernels: 0 us -> 14.7 us
  between operations: 14.1 us -> 0.89 us
  other arithmetic: 14.2 us -> 2 us
  matrix products: 9.41 us -> 2.58 us
  blocking collectives: 25.4 us -> 22.8 us
  waiting for transfers between devices: 36.2 us -> 37.8 us
    ppermute x0 -> x13, waiting for transfers between devices: none -> 33.5 us  [the longest x4 18.5 us: local(): lax.ppermute(piece, 'dp', fold)]
    ppermute x0 -> x13, starting transfers between devices: none -> 23.3 us  [the longest x4 10.3 us: local(): lax.ppermute(piece, 'dp', fold)]
    unnamed x2 -> x0, waiting for transfers between devices: 16.2 us -> none
    all_to_all x1 -> x3, waiting for transfers between devices: 20 us -> 4.28 us  [exchange(): lax.all_to_all(shaped, ('ctx', 'tp'), split_axis=0, concat_axis=0, tiled=...]
    pallas_call x0 -> x11, Pallas kernels: none -> 14.7 us  [call(): pl.pallas_call(body, out_shape=tuple(outs), in_specs=in_specs, out_specs=...]
    mul x5 -> x0, local copies, waits for them, and re-layouts: 7.5 us -> none  [the longest x2 7.11 us: local(): gate_weights[:, :, None] * grad_output[:, None, :].astype(jnp.float32)]
    dot_general x3 -> x1, matrix products: 9.41 us -> 2.58 us  [local(): jnp.dot(hidden, weight, preferred_element_type=F32).astype(BF16)]
    all_to_all x1 -> x3, starting transfers between devices: 4.56 us -> 10.8 us  [exchange(): lax.all_to_all(shaped, ('ctx', 'tp'), split_axis=0, concat_axis=0, tiled=...]
  transfers between devices with their start and end apart: 2 -> 16, of which waited for: 2 -> 9; matrix products, arithmetic and copies ran while one was open for 15% -> 4% of each run, Pallas kernels for 0% -> 9%
where the time goes in v1:
time: 122 us; the launch traced here: 121 us
  waiting for transfers between devices  37.8 us (31%)
  starting transfers between devices  34.1 us (28%)
  blocking collectives  22.8 us (19%)
  Pallas kernels  14.7 us (12%)
  local copies, waits for them, and re-layouts  6.1 us (5%)
  matrix products  2.58 us (2%)
  other arithmetic  2 us (2%)
    all_to_all x2, blocking collectives, exchange(): lax.all_to_all(shaped, ('ctx', 'tp'), split_axis=0, concat_axis=0, tiled=...  22.8 us
    ppermute x4, waiting for transfers between devices, local(): lax.ppermute(piece, 'dp', fold)  18.5 us
    ppermute x4, waiting for transfers between devices, local(): shares.append(jnp.where(at_end, lax.ppermute(give, 'dp', back), own))  15 us
    pallas_call x11, Pallas kernels, call(): pl.pallas_call(body, out_shape=tuple(outs), in_specs=in_specs, out_specs=...  14.7 us
    all_to_all x3, starting transfers between devices, exchange(): lax.all_to_all(shaped, ('ctx', 'tp'), split_axis=0, concat_axis=0, tiled=...  10.8 us
    ppermute x4, starting transfers between devices, local(): lax.ppermute(piece, 'dp', fold)  10.3 us
    unnamed x32, local copies, waits for them, and re-layouts  6.1 us
    ppermute x4, starting transfers between devices, local(): shares.append(jnp.where(at_end, lax.ppermute(give, 'dp', back), own))  5.16 us
  transfers between devices with their start and end apart: 16, of which 9 were waited for; matrix products, arithmetic and copies ran while one was open for 4% of the time, Pallas kernels for 9%

profile of v1, /device:TPU:0, one launch (start us, length us, event | category | flops | bytes accessed | tf_op | source)
XLA Modules:
  0.0 121.0 jit_solution(4943361435063498357)
XLA Ops:
  0.6 0.0 copy-start.10
  0.6 0.7 copy-done.10
  1.3 0.7 copy-done.12
  2.0 1.0 copy-done.15
  3.0 1.5 %dispatch.1 = (bf16[384,512]{1,0:T(8,128)(2,1)S(1)}, bf16[384,512]{1,0:T(8,128)(2,1)S(1)}, bf16[384,512]{1,0:T(8,128)(2,1)}, bf16[384,512]{1,0:T(8,128)(2,1)}) custom-call(s32[2,128]{1,0:T(2,128)S(1)} %bitcast.35, f32[2,128]{1,0:T(2,128)S(1)} %bitcast.37, bf16[128,2048]{1,0:T(8,128)(2,1)S(1)} %copy-done.15), custom_call_target="tpu_custom_call" | custom-call | flops 201326592 | bytes 2099200 | tf_op jit(solution)/shard_map/dispatch/pallas_call | solution.py:19
  4.5 12.7 %all_to_all.25 = bf16[8,48,512]{2,1,0:T(8,128)(2,1)S(1)} all-to-all(bf16[8,48,512]{2,1,0:T(8,128)(2,1)S(1)} %bitcast.34), channel_id=1, replica_groups=mesh['dp'=4,'ctx'=4,'tp'=2] {'ctx','tp'}, dimensions={0} | all-to-all | bytes 786432 | tf_op jit(solution)/shard_map/all_to_all | solution.py:132
  17.3 10.1 %all_to_all.26 = bf16[8,48,512]{2,1,0:T(8,128)(2,1)S(1)} all-to-all(bf16[8,48,512]{2,1,0:T(8,128)(2,1)S(1)} %bitcast.33), channel_id=1, replica_groups=mesh['dp'=4,'ctx'=4,'tp'=2] {'ctx','tp'}, dimensions={0} | all-to-all | bytes 786432 | tf_op jit(solution)/shard_map/all_to_all | solution.py:132
  27.4 3.5 %all-to-all-start.3 = ((bf16[8,48,512]{2,1,0:T(8,128)(2,1)}), bf16[8,48,512]{2,1,0:T(8,128)(2,1)S(1)}, u32[]{:S(2)}, u32[]{:S(2)}) async-start(bf16[8,48,512]{2,1,0:T(8,128)(2,1)} %bitcast.9), calls=%async_computation.3 | async-start | bytes 786432 | tf_op jit(solution)/shard_map/all_to_all | solution.py:132
  30.8 0.0 copy-done.14
  30.9 3.5 %collective-permute-start = (bf16[384,768]{1,0:T(8,128)(2,1)S(1)}, bf16[384,768]{1,0:T(8,128)(2,1)S(1)}, u32[]{:S(2)}, u32[]{:S(2)}) collective-permute-start(bf16[384,768]{1,0:T(8,128)(2,1)S(1)} %copy-done.14), channel_id=1, source_target_pairs={{0,8},{24,16},{1,9},{25,17},{2,10},{26,18},{3,11},{27,19},{4,12},{... | collective-permute-start | bytes 1769480 | tf_op jit(solution)/shard_map/ppermute | solution.py:196
  34.4 1.3 %collective-permute-start.1 = (bf16[384,512]{1,0:T(8,128)(2,1)S(1)}, bf16[384,512]{1,0:T(8,128)(2,1)S(1)}, u32[]{:S(2)}, u32[]{:S(2)}) collective-permute-start(bf16[384,512]{1,0:T(8,128)(2,1)S(1)} %bitcast.21), channel_id=1, source_target_pairs={{0,8},{24,16},{1,9},{25,17},{2,10},{26,18},{3,11},{27,19},{4,12},{... | collective-permute-start | bytes 1179656 | tf_op jit(solution)/shard_map/ppermute | solution.py:199
  35.7 2.5 %all-to-all-done.3 = bf16[8,48,512]{2,1,0:T(8,128)(2,1)S(1)} async-done(((bf16[8,48,512]{2,1,0:T(8,128)(2,1)}), bf16[8,48,512]{2,1,0:T(8,128)(2,1)S(1)}, u32[]{:S(2)}, u32[]{:S(2)}) %all-to-all-start.3) | async-done | bytes 393248 | tf_op jit(solution)/shard_map/all_to_all | solution.py:132
  38.2 3.5 %all-to-all-start.4 = ((bf16[8,48,512]{2,1,0:T(8,128)(2,1)}), bf16[8,48,512]{2,1,0:T(8,128)(2,1)S(1)}, u32[]{:S(2)}, u32[]{:S(2)}) async-start(bf16[8,48,512]{2,1,0:T(8,128)(2,1)} %bitcast.11), calls=%async_computation.4 | async-start | bytes 786432 | tf_op jit(solution)/shard_map/all_to_all | solution.py:132
  41.7 4.2 %collective-permute-start.4 = (bf16[384,512]{1,0:T(8,128)(2,1)S(1)}, bf16[384,512]{1,0:T(8,128)(2,1)}, u32[]{:S(2)}, u32[]{:S(2)}) collective-permute-start(bf16[384,512]{1,0:T(8,128)(2,1)S(1)} %bitcast.24), channel_id=1, source_target_pairs={{0,8},{24,16},{1,9},{25,17},{2,10},{26,18},{3,11},{27,19},{4,12},{... | collective-permute-start | bytes 1179656 | tf_op jit(solution)/shard_map/ppermute | solution.py:199
  45.9 1.3 %collective-permute-start.7 = (bf16[384,512]{1,0:T(8,128)(2,1)S(1)}, bf16[384,512]{1,0:T(8,128)(2,1)S(1)}, u32[]{:S(2)}, u32[]{:S(2)}) collective-permute-start(bf16[384,512]{1,0:T(8,128)(2,1)S(1)} %bitcast.27), channel_id=1, source_target_pairs={{0,8},{24,16},{1,9},{25,17},{2,10},{26,18},{3,11},{27,19},{4,12},{... | collective-permute-start | bytes 1179656 | tf_op jit(solution)/shard_map/ppermute | solution.py:199
  47.2 1.8 %all-to-all-done.4 = bf16[8,48,512]{2,1,0:T(8,128)(2,1)S(1)} async-done(((bf16[8,48,512]{2,1,0:T(8,128)(2,1)}), bf16[8,48,512]{2,1,0:T(8,128)(2,1)S(1)}, u32[]{:S(2)}, u32[]{:S(2)}) %all-to-all-start.4) | async-done | bytes 393248 | tf_op jit(solution)/shard_map/all_to_all | solution.py:132
  49.0 3.5 %collective-permute-start.10 = (bf16[384,512]{1,0:T(8,128)(2,1)S(1)}, bf16[384,512]{1,0:T(8,128)(2,1)S(1)}, u32[]{:S(2)}, u32[]{:S(2)}) collective-permute-start(bf16[384,512]{1,0:T(8,128)(2,1)S(1)} %bitcast.30), channel_id=1, source_target_pairs={{0,8},{24,16},{1,9},{25,17},{2,10},{26,18},{3,11},{27,19},{4,12},{... | collective-permute-start | bytes 1179656 | tf_op jit(solution)/shard_map/ppermute | solution.py:199
  52.5 0.0 collective-permute-done.theirs_ref
  52.5 3.9 %collective-permute-done.1.piece_theirs_ref = bf16[384,512]{1,0:T(8,128)(2,1)S(1)} collective-permute-done((bf16[384,512]{1,0:T(8,128)(2,1)S(1)}, bf16[384,512]{1,0:T(8,128)(2,1)S(1)}, u32[]{:S(2)}, u32[]{:S(2)}) %collective-permute-start.1) | collective-permute-done | bytes 393248 | tf_op jit(solution)/shard_map/ppermute | solution.py:199
  56.5 1.0 folded_parts.4
  57.5 0.7 collective-permute-start.2
  58.2 6.7 %collective-permute-done.4.piece_theirs_ref = bf16[384,512]{1,0:T(8,128)(2,1)} collective-permute-done((bf16[384,512]{1,0:T(8,128)(2,1)S(1)}, bf16[384,512]{1,0:T(8,128)(2,1)}, u32[]{:S(2)}, u32[]{:S(2)}) %collective-permute-start.4) | collective-permute-done | bytes 393248 | tf_op jit(solution)/shard_map/ppermute | solution.py:199
  64.9 2.4 %folded_parts.5 = (bf16[384,512]{1,0:T(8,128)(2,1)}, f32[384,512]{1,0:T(8,128)S(1)}) custom-call(s32[1]{0:T(128)} %bitcast.13.side_ref, bf16[384,768]{1,0:T(8,128)(2,1)S(1)} %copy-done.14, bf16[384,768]{1,0:T(8,128)(2,1)S(1)} %collective-permute-done.theirs_ref, bf16[384,512]{1,0:T(8,128)(2,1)S(1)} %bitcast.25, ...), custom_call_target="tpu_custom_call" | custom-call | flops 603979776 | bytes 3145732 | tf_op jit(solution)/shard_map/folded_parts/pallas_call | solution.py:19
  67.2 0.9 copy-done.6
  68.1 1.4 %collective-permute-start.5 = (bf16[384,512]{1,0:T(8,128)(2,1)}, bf16[384,512]{1,0:T(8,128)(2,1)}, u32[]{:S(2)}, u32[]{:S(2)}) collective-permute-start(bf16[384,512]{1,0:T(8,128)(2,1)} %get-tuple-element.32), channel_id=1, source_target_pairs={{8,16},{16,8},{9,17},{17,9},{10,18},{18,10},{11,19},{19,11},{12,20... | collective-permute-start | bytes 1179656 | tf_op jit(solution)/shard_map/ppermute | solution.py:200
  69.5 3.8 %collective-permute-done.7.piece_theirs_ref = bf16[384,512]{1,0:T(8,128)(2,1)S(1)} collective-permute-done((bf16[384,512]{1,0:T(8,128)(2,1)S(1)}, bf16[384,512]{1,0:T(8,128)(2,1)S(1)}, u32[]{:S(2)}, u32[]{:S(2)}) %collective-permute-start.7) | collective-permute-done | bytes 393248 | tf_op jit(solution)/shard_map/ppermute | solution.py:199
  73.3 1.4 %folded_parts.6 = (bf16[384,512]{1,0:T(8,128)(2,1)}, f32[384,512]{1,0:T(8,128)S(1)}) custom-call(s32[1]{0:T(128)} %bitcast.13.side_ref, bf16[384,768]{1,0:T(8,128)(2,1)S(1)} %copy-done.14, bf16[384,768]{1,0:T(8,128)(2,1)S(1)} %collective-permute-done.theirs_ref, bf16[384,512]{1,0:T(8,128)(2,1)S(1)} %bitcast.28, ...), custom_call_target="tpu_custom_call" | custom-call | flops 603979776 | bytes 3145732 | tf_op jit(solution)/shard_map/folded_parts/pallas_call | solution.py:19
  74.7 0.9 copy-done.4
  75.6 1.5 %collective-permute-start.8 = (bf16[384,512]{1,0:T(8,128)(2,1)}, bf16[384,512]{1,0:T(8,128)(2,1)}, u32[]{:S(2)}, u32[]{:S(2)}) collective-permute-start(bf16[384,512]{1,0:T(8,128)(2,1)} %get-tuple-element.36), channel_id=1, source_target_pairs={{8,16},{16,8},{9,17},{17,9},{10,18},{18,10},{11,19},{19,11},{12,20... | collective-permute-start | bytes 1179656 | tf_op jit(solution)/shard_map/ppermute | solution.py:200
  77.1 4.1 %collective-permute-done.10.piece_theirs_ref = bf16[384,512]{1,0:T(8,128)(2,1)S(1)} collective-permute-done((bf16[384,512]{1,0:T(8,128)(2,1)S(1)}, bf16[384,512]{1,0:T(8,128)(2,1)S(1)}, u32[]{:S(2)}, u32[]{:S(2)}) %collective-permute-start.10) | collective-permute-done | bytes 393248 | tf_op jit(solution)/shard_map/ppermute | solution.py:199
  81.2 1.4 %folded_parts.7 = (bf16[384,512]{1,0:T(8,128)(2,1)}, f32[384,512]{1,0:T(8,128)S(1)}) custom-call(s32[1]{0:T(128)} %bitcast.13.side_ref, bf16[384,768]{1,0:T(8,128)(2,1)S(1)} %copy-done.14, bf16[384,768]{1,0:T(8,128)(2,1)S(1)} %collective-permute-done.theirs_ref, bf16[384,512]{1,0:T(8,128)(2,1)S(1)} %bitcast.31, ...), custom_call_target="tpu_custom_call" | custom-call | flops 603979776 | bytes 3145732 | tf_op jit(solution)/shard_map/folded_parts/pallas_call | solution.py:19
  82.5 0.7 collective-permute-start.11
  83.2 0.0 collective-permute-done.2.got_ref
  83.2 0.7 finish.4
  84.0 1.3 %collective-permute-start.3 = (bf16[192,512]{1,0:T(8,128)(2,1)}, bf16[192,512]{1,0:T(8,128)(2,1)}, u32[]{:S(2)}, u32[]{:S(2)}) collective-permute-start(bf16[192,512]{1,0:T(8,128)(2,1)} %get-tuple-element.29), channel_id=1, source_target_pairs={{8,0},{16,24},{9,1},{17,25},{10,2},{18,26},{11,3},{19,27},{12,4},{... | collective-permute-start | bytes 589832 | tf_op jit(solution)/shard_map/ppermute | solution.py:201
  85.3 0.0 copy-done
  85.3 2.6 %convolution_convert_fusion = bf16[384,2048]{1,0:T(8,128)(2,1)} fusion(bf16[384,768]{1,0:T(8,128)(2,1)S(1)} %copy-done.14, bf16[1,768,2048]{2,1,0:T(8,128)(2,1)S(1)} %copy-done), kind=kOutput, calls=%fused_computation | convolution fusion | flops 1208745984 | bytes 5308416 | tf_op jit(solution)/shard_map/dot_general | solution.py:209
  87.9 0.0 copy-done.2
  87.9 0.0 copy-done.8
  87.9 3.9 %all-to-all-start = ((bf16[8,48,2048]{2,1,0:T(8,128)(2,1)}), bf16[8,48,2048]{2,1,0:T(8,128)(2,1)S(1)}, u32[]{:S(2)}, u32[]{:S(2)}) async-start(bf16[8,48,2048]{2,1,0:T(8,128)(2,1)} %bitcast.39), calls=%async_computation | async-start | bytes 3145728 | tf_op jit(solution)/shard_map/all_to_all | solution.py:132
  91.7 1.9 %copy-done.1 = bf16[1,768,2048]{2,1,0:T(8,128)(2,1)S(1)} copy-done((bf16[1,768,2048]{2,1,0:T(8,128)(2,1)S(1)}, bf16[1,768,2048]{2,1,0:T(8,128)(2,1)}, u32[]{:S(2)}) %copy-start.1) | copy-done | bytes 3145752
  93.6 2.2 %grad_rows.1 = bf16[384,768]{1,0:T(8,128)(2,1)} custom-call(bf16[768,2048]{1,0:T(8,128)(2,1)S(1)} %bitcast.20, bf16[384,512]{1,0:T(8,128)(2,1)S(1)} %bitcast.23, bf16[384,512]{1,0:T(8,128)(2,1)S(1)} %bitcast.26, bf16[384,512]{1,0:T(8,128)(2,1)S(1)} %bitcast.29, bf16[384,512]{1,0:T(8,128)(2,1)S(1)} %bitcast.32), custom_call_target="tpu_custom_call" | custom-call | flops 1207959552 | bytes 5308416 | tf_op jit(solution)/shard_map/grad_rows/pallas_call | solution.py:19
  95.9 0.0 collective-permute-done.5.got_ref
  95.9 0.0 copy-done.7
  95.9 1.2 finish.5
  97.1 1.3 %collective-permute-start.6 = (bf16[192,512]{1,0:T(8,128)(2,1)S(1)}, bf16[192,512]{1,0:T(8,128)(2,1)S(1)}, u32[]{:S(2)}, u32[]{:S(2)}) collective-permute-start(bf16[192,512]{1,0:T(8,128)(2,1)S(1)} %get-tuple-element.33), channel_id=1, source_target_pairs={{8,0},{16,24},{9,1},{17,25},{10,2},{18,26},{11,3},{19,27},{12,4},{... | collective-permute-start | bytes 589832 | tf_op jit(solution)/shard_map/ppermute | solution.py:201
  98.4 0.0 collective-permute-done.8.got_ref
  98.4 0.0 copy-done.5
  98.4 1.1 finish.6
  99.5 1.3 %collective-permute-start.9 = (bf16[192,512]{1,0:T(8,128)(2,1)S(1)}, bf16[192,512]{1,0:T(8,128)(2,1)S(1)}, u32[]{:S(2)}, u32[]{:S(2)}) collective-permute-start(bf16[192,512]{1,0:T(8,128)(2,1)S(1)} %get-tuple-element.37), channel_id=1, source_target_pairs={{8,0},{16,24},{9,1},{17,25},{10,2},{18,26},{11,3},{19,27},{12,4},{... | collective-permute-start | bytes 589832 | tf_op jit(solution)/shard_map/ppermute | solution.py:201
  100.8 0.0 collective-permute-done.11.got_ref
  100.8 0.0 copy-done.3
  100.8 0.1 finish.7
  100.9 1.3 %collective-permute-start.12 = (bf16[192,512]{1,0:T(8,128)(2,1)S(1)}, bf16[192,512]{1,0:T(8,128)(2,1)S(1)}, u32[]{:S(2)}, u32[]{:S(2)}) collective-permute-start(bf16[192,512]{1,0:T(8,128)(2,1)S(1)} %get-tuple-element.41), channel_id=1, source_target_pairs={{8,0},{16,24},{9,1},{17,25},{10,2},{18,26},{11,3},{19,27},{12,4},{... | collective-permute-start | bytes 589832 | tf_op jit(solution)/shard_map/ppermute | solution.py:201
  102.2 0.0 collective-permute-done.3
  102.2 0.0 copy-done.9
  102.2 1.0 broadcast_select_fusion.3
  103.2 6.8 %collective-permute-done.6 = bf16[192,512]{1,0:T(8,128)(2,1)S(1)} collective-permute-done((bf16[192,512]{1,0:T(8,128)(2,1)S(1)}, bf16[192,512]{1,0:T(8,128)(2,1)S(1)}, u32[]{:S(2)}, u32[]{:S(2)}) %collective-permute-start.6) | collective-permute-done | bytes 196640 | tf_op jit(solution)/shard_map/ppermute | solution.py:201
  110.1 4.2 %collective-permute-done.9 = bf16[192,512]{1,0:T(8,128)(2,1)S(1)} collective-permute-done((bf16[192,512]{1,0:T(8,128)(2,1)S(1)}, bf16[192,512]{1,0:T(8,128)(2,1)S(1)}, u32[]{:S(2)}, u32[]{:S(2)}) %collective-permute-start.9) | collective-permute-done | bytes 196640 | tf_op jit(solution)/shard_map/ppermute | solution.py:201
  114.3 4.0 %collective-permute-done.12 = bf16[192,512]{1,0:T(8,128)(2,1)S(1)} collective-permute-done((bf16[192,512]{1,0:T(8,128)(2,1)S(1)}, bf16[192,512]{1,0:T(8,128)(2,1)S(1)}, u32[]{:S(2)}, u32[]{:S(2)}) %collective-permute-start.12) | collective-permute-done | bytes 196640 | tf_op jit(solution)/shard_map/ppermute | solution.py:201
  118.3 1.0 maximum_bitcast_fusion
  119.3 0.0 all-to-all-done
  119.3 0.0 copy-done.11
  119.3 1.7 %combine.1 = bf16[128,2048]{1,0:T(8,128)(2,1)} custom-call(s32[2,128]{1,0:T(2,128)S(1)} %bitcast.36, f32[2,128]{1,0:T(2,128)S(1)} %bitcast.38, bf16[384,2048]{1,0:T(8,128)(2,1)S(1)} %bitcast.19), custom_call_target="tpu_custom_call" | custom-call | flops 402653184 | bytes 2099200 | tf_op jit(solution)/shard_map/combine/pallas_call | solution.py:19
  (19 shorter events, 0.1 us)
Async XLA Ops:
  0.6 0.7 copy-start.10
  1.3 0.7 copy-start.12
  2.0 1.0 copy-start.15
  3.0 27.8 %copy-start.14 = (bf16[384,768]{1,0:T(8,128)(2,1)S(1)}, bf16[384,768]{1,0:T(8,128)(2,1)}, u32[]{:S(2)}) copy-start(bf16[384,768]{1,0:T(8,128)(2,1)} %mine_ref.7) | copy-start | bytes 1769476
  27.4 10.8 %all-to-all-start.3 = ((bf16[8,48,512]{2,1,0:T(8,128)(2,1)}), bf16[8,48,512]{2,1,0:T(8,128)(2,1)S(1)}, u32[]{:S(2)}, u32[]{:S(2)}) async-start(bf16[8,48,512]{2,1,0:T(8,128)(2,1)} %bitcast.9), calls=%async_computation.3 | async-start | bytes 786432 | tf_op jit(solution)/shard_map/all_to_all | solution.py:132
  30.9 21.7 %collective-permute-start = (bf16[384,768]{1,0:T(8,128)(2,1)S(1)}, bf16[384,768]{1,0:T(8,128)(2,1)S(1)}, u32[]{:S(2)}, u32[]{:S(2)}) collective-permute-start(bf16[384,768]{1,0:T(8,128)(2,1)S(1)} %copy-done.14), channel_id=1, source_target_pairs={{0,8},{24,16},{1,9},{25,17},{2,10},{26,18},{3,11},{27,19},{4,12},{... | collective-permute-start | bytes 1769480 | tf_op jit(solution)/shard_map/ppermute | solution.py:196
  34.4 22.0 %collective-permute-start.1 = (bf16[384,512]{1,0:T(8,128)(2,1)S(1)}, bf16[384,512]{1,0:T(8,128)(2,1)S(1)}, u32[]{:S(2)}, u32[]{:S(2)}) collective-permute-start(bf16[384,512]{1,0:T(8,128)(2,1)S(1)} %bitcast.21), channel_id=1, source_target_pairs={{0,8},{24,16},{1,9},{25,17},{2,10},{26,18},{3,11},{27,19},{4,12},{... | collective-permute-start | bytes 1179656 | tf_op jit(solution)/shard_map/ppermute | solution.py:199
  38.2 10.8 %all-to-all-start.4 = ((bf16[8,48,512]{2,1,0:T(8,128)(2,1)}), bf16[8,48,512]{2,1,0:T(8,128)(2,1)S(1)}, u32[]{:S(2)}, u32[]{:S(2)}) async-start(bf16[8,48,512]{2,1,0:T(8,128)(2,1)} %bitcast.11), calls=%async_computation.4 | async-start | bytes 786432 | tf_op jit(solution)/shard_map/all_to_all | solution.py:132
  41.7 23.2 %collective-permute-start.4 = (bf16[384,512]{1,0:T(8,128)(2,1)S(1)}, bf16[384,512]{1,0:T(8,128)(2,1)}, u32[]{:S(2)}, u32[]{:S(2)}) collective-permute-start(bf16[384,512]{1,0:T(8,128)(2,1)S(1)} %bitcast.24), channel_id=1, source_target_pairs={{0,8},{24,16},{1,9},{25,17},{2,10},{26,18},{3,11},{27,19},{4,12},{... | collective-permute-start | bytes 1179656 | tf_op jit(solution)/shard_map/ppermute | solution.py:199
  45.9 27.4 %collective-permute-start.7 = (bf16[384,512]{1,0:T(8,128)(2,1)S(1)}, bf16[384,512]{1,0:T(8,128)(2,1)S(1)}, u32[]{:S(2)}, u32[]{:S(2)}) collective-permute-start(bf16[384,512]{1,0:T(8,128)(2,1)S(1)} %bitcast.27), channel_id=1, source_target_pairs={{0,8},{24,16},{1,9},{25,17},{2,10},{26,18},{3,11},{27,19},{4,12},{... | collective-permute-start | bytes 1179656 | tf_op jit(solution)/shard_map/ppermute | solution.py:199
  49.0 32.2 %collective-permute-start.10 = (bf16[384,512]{1,0:T(8,128)(2,1)S(1)}, bf16[384,512]{1,0:T(8,128)(2,1)S(1)}, u32[]{:S(2)}, u32[]{:S(2)}) collective-permute-start(bf16[384,512]{1,0:T(8,128)(2,1)S(1)} %bitcast.30), channel_id=1, source_target_pairs={{0,8},{24,16},{1,9},{25,17},{2,10},{26,18},{3,11},{27,19},{4,12},{... | collective-permute-start | bytes 1179656 | tf_op jit(solution)/shard_map/ppermute | solution.py:199
  57.5 25.8 %collective-permute-start.2 = (bf16[384,512]{1,0:T(8,128)(2,1)S(1)}, bf16[384,512]{1,0:T(8,128)(2,1)S(1)}, u32[]{:S(2)}, u32[]{:S(2)}) collective-permute-start(bf16[384,512]{1,0:T(8,128)(2,1)S(1)} %get-tuple-element.28), channel_id=1, source_target_pairs={{8,16},{16,8},{9,17},{17,9},{10,18},{18,10},{11,19},{19,11},{12,20... | collective-permute-start | bytes 1179656 | tf_op jit(solution)/shard_map/ppermute | solution.py:200
  67.2 0.9 copy-start.6
  68.1 27.7 %collective-permute-start.5 = (bf16[384,512]{1,0:T(8,128)(2,1)}, bf16[384,512]{1,0:T(8,128)(2,1)}, u32[]{:S(2)}, u32[]{:S(2)}) collective-permute-start(bf16[384,512]{1,0:T(8,128)(2,1)} %get-tuple-element.32), channel_id=1, source_target_pairs={{8,16},{16,8},{9,17},{17,9},{10,18},{18,10},{11,19},{19,11},{12,20... | collective-permute-start | bytes 1179656 | tf_op jit(solution)/shard_map/ppermute | solution.py:200
  74.7 0.9 copy-start.4
  75.6 9.7 %copy-start = (bf16[1,768,2048]{2,1,0:T(8,128)(2,1)S(1)}, bf16[1,768,2048]{2,1,0:T(8,128)(2,1)}, u32[]{:S(2)}) copy-start(bf16[1,768,2048]{2,1,0:T(8,128)(2,1)} %param.9) | copy-start | bytes 9437188
  75.6 22.8 %collective-permute-start.8 = (bf16[384,512]{1,0:T(8,128)(2,1)}, bf16[384,512]{1,0:T(8,128)(2,1)}, u32[]{:S(2)}, u32[]{:S(2)}) collective-permute-start(bf16[384,512]{1,0:T(8,128)(2,1)} %get-tuple-element.36), channel_id=1, source_target_pairs={{8,16},{16,8},{9,17},{17,9},{10,18},{18,10},{11,19},{19,11},{12,20... | collective-permute-start | bytes 1179656 | tf_op jit(solution)/shard_map/ppermute | solution.py:200
  82.5 5.3 %copy-start.2 = (f32[384,512]{1,0:T(8,128)}, f32[384,512]{1,0:T(8,128)S(1)}, u32[]{:S(2)}) copy-start(f32[384,512]{1,0:T(8,128)S(1)} %get-tuple-element.39.keep_ref) | copy-start | bytes 2359300
  82.5 18.2 %collective-permute-start.11 = (bf16[384,512]{1,0:T(8,128)(2,1)}, bf16[384,512]{1,0:T(8,128)(2,1)S(1)}, u32[]{:S(2)}, u32[]{:S(2)}) collective-permute-start(bf16[384,512]{1,0:T(8,128)(2,1)} %get-tuple-element.40), channel_id=1, source_target_pairs={{8,16},{16,8},{9,17},{17,9},{10,18},{18,10},{11,19},{19,11},{12,20... | collective-permute-start | bytes 1179656 | tf_op jit(solution)/shard_map/ppermute | solution.py:200
  84.0 3.9 %copy-start.8 = (bf16[192,512]{1,0:T(8,128)(2,1)}, bf16[192,512]{1,0:T(8,128)(2,1)S(1)}, u32[]{:S(2)}) copy-start(bf16[192,512]{1,0:T(8,128)(2,1)S(1)} %get-tuple-element.30) | copy-start | bytes 589828
  84.0 18.2 %collective-permute-start.3 = (bf16[192,512]{1,0:T(8,128)(2,1)}, bf16[192,512]{1,0:T(8,128)(2,1)}, u32[]{:S(2)}, u32[]{:S(2)}) collective-permute-start(bf16[192,512]{1,0:T(8,128)(2,1)} %get-tuple-element.29), channel_id=1, source_target_pairs={{8,0},{16,24},{9,1},{17,25},{10,2},{18,26},{11,3},{19,27},{12,4},{... | collective-permute-start | bytes 589832 | tf_op jit(solution)/shard_map/ppermute | solution.py:201
  87.9 31.4 %all-to-all-start = ((bf16[8,48,2048]{2,1,0:T(8,128)(2,1)}), bf16[8,48,2048]{2,1,0:T(8,128)(2,1)S(1)}, u32[]{:S(2)}, u32[]{:S(2)}) async-start(bf16[8,48,2048]{2,1,0:T(8,128)(2,1)} %bitcast.39), calls=%async_computation | async-start | bytes 3145728 | tf_op jit(solution)/shard_map/all_to_all | solution.py:132
  91.7 1.9 %copy-start.1 = (bf16[1,768,2048]{2,1,0:T(8,128)(2,1)S(1)}, bf16[1,768,2048]{2,1,0:T(8,128)(2,1)}, u32[]{:S(2)}) copy-start(bf16[1,768,2048]{2,1,0:T(8,128)(2,1)} %param.9) | copy-start | bytes 9437188
  93.6 2.3 %copy-start.7 = (f32[384,512]{1,0:T(8,128)S(1)}, f32[384,512]{1,0:T(8,128)}, u32[]{:S(2)}) copy-start(f32[384,512]{1,0:T(8,128)} %copy-done.6) | copy-start | bytes 2359300
  93.6 4.7 %copy-start.5 = (f32[384,512]{1,0:T(8,128)S(1)}, f32[384,512]{1,0:T(8,128)}, u32[]{:S(2)}) copy-start(f32[384,512]{1,0:T(8,128)} %copy-done.4) | copy-start | bytes 2359300
  95.9 4.9 %copy-start.3 = (f32[384,512]{1,0:T(8,128)S(1)}, f32[384,512]{1,0:T(8,128)}, u32[]{:S(2)}) copy-start(f32[384,512]{1,0:T(8,128)} %copy-done.2) | copy-start | bytes 2359300
  95.9 6.3 %copy-start.9 = (bf16[192,512]{1,0:T(8,128)(2,1)S(1)}, bf16[192,512]{1,0:T(8,128)(2,1)}, u32[]{:S(2)}) copy-start(bf16[192,512]{1,0:T(8,128)(2,1)} %copy-done.8) | copy-start | bytes 589828
  97.1 13.0 %collective-permute-start.6 = (bf16[192,512]{1,0:T(8,128)(2,1)S(1)}, bf16[192,512]{1,0:T(8,128)(2,1)S(1)}, u32[]{:S(2)}, u32[]{:S(2)}) collective-permute-start(bf16[192,512]{1,0:T(8,128)(2,1)S(1)} %get-tuple-element.33), channel_id=1, source_target_pairs={{8,0},{16,24},{9,1},{17,25},{10,2},{18,26},{11,3},{19,27},{12,4},{... | collective-permute-start | bytes 589832 | tf_op jit(solution)/shard_map/ppermute | solution.py:201
  99.5 14.8 %collective-permute-start.9 = (bf16[192,512]{1,0:T(8,128)(2,1)S(1)}, bf16[192,512]{1,0:T(8,128)(2,1)S(1)}, u32[]{:S(2)}, u32[]{:S(2)}) collective-permute-start(bf16[192,512]{1,0:T(8,128)(2,1)S(1)} %get-tuple-element.37), channel_id=1, source_target_pairs={{8,0},{16,24},{9,1},{17,25},{10,2},{18,26},{11,3},{19,27},{12,4},{... | collective-permute-start | bytes 589832 | tf_op jit(solution)/shard_map/ppermute | solution.py:201
  100.9 17.4 %collective-permute-start.12 = (bf16[192,512]{1,0:T(8,128)(2,1)S(1)}, bf16[192,512]{1,0:T(8,128)(2,1)S(1)}, u32[]{:S(2)}, u32[]{:S(2)}) collective-permute-start(bf16[192,512]{1,0:T(8,128)(2,1)S(1)} %get-tuple-element.41), channel_id=1, source_target_pairs={{8,0},{16,24},{9,1},{17,25},{10,2},{18,26},{11,3},{19,27},{12,4},{... | collective-permute-start | bytes 589832 | tf_op jit(solution)/shard_map/ppermute | solution.py:201
  110.0 9.3 %copy-start.11 = (s32[128,2]{0,1:T(2,128)S(1)}, s32[128,2]{0,1:T(2,128)}, u32[]{:S(2)}) copy-start(s32[128,2]{0,1:T(2,128)} %param.7) | copy-start | bytes 3076
  110.0 9.3 %copy-start.13 = (f32[128,2]{0,1:T(2,128)S(1)}, f32[128,2]{0,1:T(2,128)}, u32[]{:S(2)}) copy-start(f32[128,2]{0,1:T(2,128)} %param.8) | copy-start | bytes 3076

commit v2 on v1

v2 whole, which is shorter than its diff:
```python
import jax
import jax.numpy as jnp
from jax import lax
from jax.experimental import pallas as pl
from jax.experimental.pallas import tpu as pltpu
from jax.sharding import PartitionSpec as P

grad_scale = 0.015625
PARTS = ((4,), (6, 6))
F32 = jnp.float32
BF16 = jnp.bfloat16
GROUP = ("ctx", "tp")


def call(body, outs, ins, name, flops=0, smem=0, scratch=(), in_hbm=(), out_hbm=()):
    in_specs = [
        pl.BlockSpec(memory_space=pltpu.SMEM if i < smem else pltpu.HBM if i in in_hbm else pltpu.VMEM)
        for i in range(len(ins))
    ]
    return pl.pallas_call(
        body,
        out_shape=tuple(outs),
        in_specs=in_specs,
        out_specs=tuple(
            pl.BlockSpec(memory_space=pltpu.HBM if i in out_hbm else pltpu.VMEM) for i in range(len(outs))
        ),
        scratch_shapes=scratch,
        name=name,
        cost_estimate=pl.CostEstimate(flops=0, bytes_accessed=0, transcendentals=0),
        compiler_params=pltpu.CompilerParams(vmem_limit_bytes=14 * 2**20),
    )(*ins)


def like(shape, dtype=BF16):
    return jax.ShapeDtypeStruct(shape, dtype)


def iota(shape, axis):
    return lax.broadcasted_iota(jnp.int32, shape, axis)


def after(x, *others):
    return lax.optimization_barrier((x, others))[0]


def exchange(x, experts):
    shaped = x.reshape(experts, -1, x.shape[1])
    return lax.all_to_all(shaped, GROUP, split_axis=0, concat_axis=0, tiled=True).reshape(x.shape)


def slot_rows(ids, experts, capacity):
    choices, tokens = ids.shape
    named = [(iota((experts, tokens), 0) == ids[k : k + 1]).astype(F32) for k in range(choices)]
    before = (iota((tokens, tokens), 0) < iota((tokens, tokens), 1)).astype(BF16)
    earlier = jnp.dot(sum(named).astype(BF16), before, preferred_element_type=F32)
    slots = []
    for k in range(choices):
        rank = jnp.sum(named[k] * earlier, axis=0, keepdims=True)
        slots.append(ids[k : k + 1] * capacity + rank.astype(jnp.int32))
        earlier = earlier + named[k]
    return slots


def dispatch(ids, gates, grads, experts, capacity, widths):
    choices, tokens = ids.shape
    rows = experts * capacity

    def body(ids_hbm, gates_hbm, grads_hbm, *refs):
        *out_refs, ids_ref, gates_ref, grads_ref, sems = refs
        copies = [
            pltpu.make_async_copy(src, dst, sems.at[i])
            for i, (src, dst) in enumerate(
                ((ids_hbm, ids_ref), (gates_hbm, gates_ref), (grads_hbm, grads_ref))
            )
        ]
        for copy in copies:
            copy.start()
        copies[0].wait()
        slots = slot_rows(ids_ref[...], experts, capacity)
        copies[1].wait()
        pick = jnp.zeros((rows, tokens), F32)
        scale = jnp.zeros((rows, 1), F32)
        for k in range(choices):
            hit = iota((rows, tokens), 0) == slots[k]
            pick = pick + hit.astype(F32)
            scale = scale + jnp.sum(jnp.where(hit, gates_ref[k : k + 1, :], 0.0), axis=1, keepdims=True)
        pick = pick.astype(BF16)
        copies[2].wait()
        start = 0
        for ref, width in zip(out_refs, widths):
            chosen = jnp.dot(pick, grads_ref[:, start : start + width], preferred_element_type=F32)
            ref[...] = (chosen * scale).astype(BF16)
            start += width

    return call(
        body,
        [like((rows, w)) for w in widths],
        [ids, gates, grads],
        "dispatch",
        2 * rows * tokens * sum(widths),
        in_hbm=(0, 1, 2),
        scratch=[
            pltpu.VMEM(ids.shape, ids.dtype),
            pltpu.VMEM(gates.shape, gates.dtype),
            pltpu.VMEM(grads.shape, grads.dtype),
            pltpu.SemaphoreType.DMA((3,)),
        ],
    )


def combine(ids, gates, returned, experts, capacity):
    choices, tokens = ids.shape
    rows, width = returned.shape

    def body(ids_ref, gates_ref, returned_ref, out_ref):
        slots = slot_rows(ids_ref[...], experts, capacity)
        same = iota((tokens, tokens), 0) == iota((tokens, tokens), 1)
        picks, scales = [], []
        for k in range(choices):
            slot = jnp.sum(jnp.where(same, slots[k], 0), axis=1, keepdims=True)
            picks.append((iota((tokens, rows), 1) == slot).astype(F32).astype(BF16))
            scales.append(jnp.sum(jnp.where(same, gates_ref[k : k + 1, :], 0.0), axis=1, keepdims=True))
        step = min(512, width)
        for start in range(0, width, step):
            block = returned_ref[:, start : start + step]
            out_ref[:, start : start + step] = sum(
                jnp.dot(p, block, preferred_element_type=F32) * s for p, s in zip(picks, scales)
            ).astype(BF16)

    return call(
        body,
        [like((tokens, width))],
        [ids, gates, returned],
        "combine",
        2 * choices * rows * tokens * width,
    )[0]


def expert_rows(rows, weight):
    width = weight.shape[1]
    step = min(512, width)

    def body(rows_ref, weight_ref, out_hbm, out_ref, sems):
        copies = []
        for i, start in enumerate(range(0, width, step)):
            columns = slice(start, start + step)
            out_ref[:, columns] = jnp.dot(
                rows_ref[...], weight_ref[:, columns], preferred_element_type=F32
            ).astype(BF16)
            copies.append(pltpu.make_async_copy(out_ref.at[:, columns], out_hbm.at[:, columns], sems.at[i]))
            copies[-1].start()
        for copy in copies:
            copy.wait()

    out = like((rows.shape[0], width))
    return call(
        body,
        [out],
        [rows, weight],
        "expert_rows",
        2 * rows.shape[0] * weight.size,
        out_hbm=(0,),
        scratch=[pltpu.VMEM(out.shape, out.dtype), pltpu.SemaphoreType.DMA((width // step,))],
    )[0]


def grad_rows(pieces, weight):
    rows, hidden_units = pieces[0].shape[0], weight.shape[0]

    def body(weight_ref, *refs):
        *piece_refs, out_ref = refs
        total, start = None, 0
        for ref in piece_refs:
            width = ref.shape[1]
            part = lax.dot_general(
                ref[...],
                weight_ref[:, start : start + width],
                (((1,), (1,)), ((), ())),
                preferred_element_type=F32,
            )
            total = part if total is None else total + part
            start += width
        out_ref[...] = total.astype(BF16)

    return call(
        body,
        [like((rows, hidden_units))],
        [weight, *pieces],
        "grad_rows",
        2 * rows * weight.size,
    )[0]


def folded_parts(spot, mine, theirs, piece, piece_theirs):
    half, width = mine.shape[1] // 2, piece.shape[1]

    def body(spot_ref, mine_ref, theirs_ref, piece_ref, piece_theirs_ref, give_ref, keep_hbm, keep_ref, sem):
        def rows(which):
            columns = pl.ds(pl.multiple_of(which * half, half), half)
            return sum(
                lax.dot_general(h[:, columns], p[...], (((0,), (0,)), ((), ())), preferred_element_type=F32)
                for h, p in ((mine_ref, piece_ref), (theirs_ref, piece_theirs_ref))
            )

        keep_ref[...] = rows(spot_ref[0]).astype(BF16)
        copy = pltpu.make_async_copy(keep_ref, keep_hbm, sem)
        copy.start()
        give_ref[...] = rows(1 - spot_ref[0]).astype(BF16)
        copy.wait()

    return call(
        body,
        [like((half, width))] * 2,
        [spot, mine, theirs, piece, piece_theirs],
        "folded_parts",
        8 * mine.shape[0] * half * width,
        smem=1,
        out_hbm=(1,),
        scratch=[pltpu.VMEM((half, width), BF16), pltpu.SemaphoreType.DMA],
    )


def finish(spot, keep, got):
    half, width = keep.shape
    share = half // 2

    def body(spot_ref, keep_ref, got_ref, own_ref, give_ref):
        def rows(which):
            at = pl.ds(pl.multiple_of(which * share, share), share)
            return ((keep_ref[at, :].astype(F32) + got_ref[at, :].astype(F32)) * grad_scale).astype(BF16)

        give_ref[...] = rows(spot_ref[0])
        own_ref[...] = rows(1 - spot_ref[0])

    return call(body, [like((share, width))] * 2, [spot, keep, got], "finish", smem=1)


def shares(spot, own, handed):
    rows, width = own[0].shape[0], sum(x.shape[1] for x in own)

    def body(spot_ref, *refs):
        *in_refs, out_ref = refs
        at_end, start = spot_ref[1] != 0, 0
        for own_ref, handed_ref in zip(in_refs[: len(own)], in_refs[len(own) :]):
            columns = slice(start, start + own_ref.shape[1])
            out_ref[:, columns] = jnp.where(at_end, handed_ref[...], own_ref[...])
            start += own_ref.shape[1]

    return call(body, [like((rows, width))], [spot, *own, *handed], "shares", smem=1)[0]


def local(hidden, grad_output, expert_ids, gate_weights, w_down):
    replicas = lax.axis_size("dp")
    experts = lax.axis_size("ctx") * lax.axis_size("tp")
    capacity = hidden.shape[0] // experts
    width = grad_output.shape[1]
    weight = w_down[0]
    ids, gates = expert_ids.T, gate_weights.T
    widths = [[p * width // 16 for p in cuts] for cuts in PARTS]
    line = replicas == 4
    fold, swap, back = [(0, 1), (3, 2)], [(1, 2), (2, 1)], [(1, 0), (2, 3)]

    theirs = lax.ppermute(hidden, "dp", fold) if line else hidden
    outgoing = dispatch(ids, gates, grad_output, experts, capacity, [sum(w) for w in widths])
    expert_out = expert_rows(hidden, weight)
    if not line:
        pieces = [exchange(x, experts) for x in outgoing]
        returned = exchange(expert_out, experts)
        incoming = jnp.concatenate(pieces, axis=1)
        part = lax.dot_general(hidden, incoming, (((0,), (0,)), ((), ())), preferred_element_type=F32)
        summed = lax.psum_scatter(part.astype(BF16), "dp", scatter_dimension=0, tiled=True)
        grad_down = (summed.astype(F32) * grad_scale).astype(BF16)
        combined = combine(ids, gates, returned, experts, capacity)
        return (combined, grad_rows(pieces, weight), grad_down[None])

    place = lax.axis_index("dp")
    at_end = (place == 0) | (place == replicas - 1)
    spot = jnp.stack([(2 * place >= replicas).astype(jnp.int32), at_end.astype(jnp.int32)])

    first = exchange(outgoing[0], experts)
    pieces, folded = [first], [lax.ppermute(first, "dp", fold)]
    give, keep = folded_parts(spot, hidden, theirs, pieces[0], folded[0])
    gives, keeps = [give], [keep]
    arrived = after(exchange(after(outgoing[1], expert_out, theirs), experts), give)
    start = 0
    for cut in widths[1]:
        pieces.append(arrived[:, start : start + cut])
        folded.append(lax.ppermute(pieces[-1], "dp", fold))
        start += cut
    last = len(pieces) - 1
    got = [lax.ppermute(give, "dp", swap)]
    returned = exchange(after(expert_out, pieces[-1], give), experts)
    folded[1] = after(folded[1], got[0])
    for i in range(1, last + 1):
        give, keep = folded_parts(spot, hidden, theirs, pieces[i], folded[i])
        gives.append(give)
        keeps.append(keep)
        got.append(lax.ppermute(give, "dp", swap))

    got[:last] = after(tuple(got[:last]), gives[-1])
    grad_hidden = grad_rows(list(after(tuple(pieces), gives[-1])), weight)
    got[-1] = after(got[-1], grad_hidden)
    formed, handed = [], []
    for i in range(last + 1):
        own, give = finish(spot, keeps[i], got[i])
        formed.append(own)
        handed.append(lax.ppermute(give, "dp", back))
        if i < last:
            got[-1] = after(got[-1], handed[-1])
    combined = combine(ids, gates, returned, experts, capacity)
    grad_down = shares(spot, formed, handed)
    return (combined, grad_hidden, grad_down[None])


def solution(mesh):
    rows = P(("dp", "ctx", "tp"), None)
    return jax.shard_map(
        local,
        mesh=mesh,
        in_specs=(rows, rows, rows, rows, P(("ctx", "tp"), None, None)),
        out_specs=(rows, rows, P(("ctx", "tp"), "dp", None)),
        check_vma=False,
    )
```

time: 122 us -> 105 us (0.86)
  blocking collectives: 22.8 us -> 0 us
  Pallas kernels: 14.7 us -> 22.7 us
  matrix products: 2.58 us -> 0 us
  local copies, waits for them, and re-layouts: 6.1 us -> 8.39 us
  other arithmetic: 2 us -> 0.08 us
  starting transfers between devices: 34.1 us -> 32.2 us
  waiting for transfers between devices: 37.8 us -> 39.5 us
    all_to_all x2 -> x0, blocking collectives: 22.8 us -> none  [exchange(): lax.all_to_all(shaped, ('ctx', 'tp'), split_axis=0, concat_axis=0, tiled=...]
    pallas_call x11, Pallas kernels: 14.7 us -> 22.7 us  [call(): pl.pallas_call(body, out_shape=tuple(outs), in_specs=in_specs, out_specs=...]
    ppermute x13 -> x10, starting transfers between devices: 23.3 us -> 20.4 us  [the longest x2 6.59 us: local(): folded.append(lax.ppermute(pieces[-1], 'dp', fold))]
    dot_general x1 -> x0, matrix products: 2.58 us -> none  [local(): jnp.dot(hidden, weight, preferred_element_type=F32).astype(BF16)]
    slice x0 -> x1, local copies, waits for them, and re-layouts: none -> 2.13 us  [local(): pieces.append(arrived[:, start:start + cut])]
    ppermute x13 -> x10, waiting for transfers between devices: 33.5 us -> 35.3 us  [the longest x3 14.9 us: local(): handed.append(lax.ppermute(give, 'dp', back))]
    unnamed x32 -> x30, local copies, waits for them, and re-layouts: 6.1 us -> 6.26 us
  transfers between devices with their start and end apart: 16 -> 13, of which waited for: 9 -> 7; matrix products, arithmetic and copies ran while one was open for 4% -> 0% of each run, Pallas kernels for 9% -> 20%
where the time goes in v2:
time: 105 us; the launch traced here: 104 us
  waiting for transfers between devices  39.5 us (38%)
  starting transfers between devices  32.2 us (31%)
  Pallas kernels  22.7 us (22%)
  local copies, waits for them, and re-layouts  8.39 us (8%)
    pallas_call x11, Pallas kernels, call(): pl.pallas_call(body, out_shape=tuple(outs), in_specs=in_specs, out_specs=...  22.7 us
    ppermute x3, waiting for transfers between devices, local(): handed.append(lax.ppermute(give, 'dp', back))  14.9 us
    all_to_all x3, starting transfers between devices, exchange(): lax.all_to_all(shaped, GROUP, split_axis=0, concat_axis=0, tiled=True)  11.8 us
    ppermute x2, waiting for transfers between devices, local(): folded.append(lax.ppermute(pieces[-1], 'dp', fold))  11.6 us
    ppermute x1, waiting for transfers between devices, local(): pieces, folded = ([first], [lax.ppermute(first, 'dp', fold)])  8.79 us
    ppermute x2, starting transfers between devices, local(): folded.append(lax.ppermute(pieces[-1], 'dp', fold))  6.59 us
    unnamed x30, local copies, waits for them, and re-layouts  6.26 us
    ppermute x1, starting transfers between devices, local(): theirs = lax.ppermute(hidden, 'dp', fold) if line else hidden  5.1 us
  transfers between devices with their start and end apart: 13, of which 7 were waited for; matrix products, arithmetic and copies ran while one was open for 0% of the time, Pallas kernels for 20%

profile of v2, /device:TPU:0, one launch (start us, length us, event | category | flops | bytes accessed | tf_op | source)
XLA Modules:
  0.0 103.9 jit_solution(7275894812647354759)
XLA Ops:
  0.6 0.0 copy-start.2
  0.6 5.1 %collective-permute-start = (bf16[384,768]{1,0:T(8,128)(2,1)}, bf16[384,768]{1,0:T(8,128)(2,1)S(1)}, u32[]{:S(2)}, u32[]{:S(2)}) collective-permute-start(bf16[384,768]{1,0:T(8,128)(2,1)} %mine_ref.5), channel_id=1, source_target_pairs={{0,8},{24,16},{1,9},{25,17},{2,10},{26,18},{3,11},{27,19},{4,12},{... | collective-permute-start | bytes 1769480 | tf_op jit(solution)/shard_map/ppermute | solution.py:263
  5.7 0.0 copy-start.6
  5.8 1.0 copy-done.6
  6.8 0.7 copy-done.11
  7.5 0.7 copy-done.13
  8.1 2.0 %dispatch.1 = (bf16[384,512]{1,0:T(8,128)(2,1)}, bf16[384,1536]{1,0:T(8,128)(2,1)}) custom-call(s32[2,128]{1,0:T(2,128)S(1)} %bitcast.19, f32[2,128]{1,0:T(2,128)S(1)} %bitcast.21, bf16[128,2048]{1,0:T(8,128)(2,1)S(1)} %copy-done.6), custom_call_target="tpu_custom_call" | custom-call | tf_op jit(solution)/shard_map/dispatch/pallas_call | solution.py:20
  10.1 3.7 %all-to-all-start.1 = ((bf16[8,48,512]{2,1,0:T(8,128)(2,1)}), bf16[8,48,512]{2,1,0:T(8,128)(2,1)S(1)}, u32[]{:S(2)}, u32[]{:S(2)}) async-start(bf16[8,48,512]{2,1,0:T(8,128)(2,1)} %bitcast.7), calls=%async_computation.1 | async-start | bytes 786432 | tf_op jit(solution)/shard_map/all_to_all | solution.py:48
  13.9 0.0 copy-done.2
  13.9 0.0 copy-start
  13.9 1.9 %copy-done = bf16[1,768,2048]{2,1,0:T(8,128)(2,1)S(1)} copy-done((bf16[1,768,2048]{2,1,0:T(8,128)(2,1)S(1)}, bf16[1,768,2048]{2,1,0:T(8,128)(2,1)}, u32[]{:S(2)}) %copy-start) | copy-done | bytes 3145752
  15.8 2.1 %expert_rows.1 = bf16[384,2048]{1,0:T(8,128)(2,1)S(1)} custom-call(bf16[384,768]{1,0:T(8,128)(2,1)S(1)} %copy-done.2, bf16[768,2048]{1,0:T(8,128)(2,1)S(1)} %bitcast.12), custom_call_target="tpu_custom_call" | custom-call | tf_op jit(solution)/shard_map/expert_rows/pallas_call | solution.py:20
  17.9 0.0 copy-start.3
  17.9 1.2 %copy-done.3 = bf16[384,2048]{1,0:T(8,128)(2,1)} copy-done((bf16[384,2048]{1,0:T(8,128)(2,1)}, bf16[384,2048]{1,0:T(8,128)(2,1)S(1)}, u32[]{:S(2)}) %copy-start.3) | copy-done | bytes 1572888
  19.1 0.0 collective-permute-done.theirs_ref
  19.1 2.2 %all-to-all-done.1 = bf16[8,48,512]{2,1,0:T(8,128)(2,1)S(1)} async-done(((bf16[8,48,512]{2,1,0:T(8,128)(2,1)}), bf16[8,48,512]{2,1,0:T(8,128)(2,1)S(1)}, u32[]{:S(2)}, u32[]{:S(2)}) %all-to-all-start.1) | async-done | bytes 393248 | tf_op jit(solution)/shard_map/all_to_all | solution.py:48
  21.3 4.3 %all-to-all-start = ((bf16[8,48,1536]{2,1,0:T(8,128)(2,1)}), bf16[8,48,1536]{2,1,0:T(8,128)(2,1)}, u32[]{:S(2)}, u32[]{:S(2)}) async-start(bf16[8,48,1536]{2,1,0:T(8,128)(2,1)} %bitcast.3), calls=%async_computation | async-start | bytes 2359296 | tf_op jit(solution)/shard_map/all_to_all | solution.py:48
  25.6 1.6 %collective-permute-start.1 = (bf16[384,512]{1,0:T(8,128)(2,1)S(1)}, bf16[384,512]{1,0:T(8,128)(2,1)S(1)}, u32[]{:S(2)}, u32[]{:S(2)}) collective-permute-start(bf16[384,512]{1,0:T(8,128)(2,1)S(1)} %bitcast.16), channel_id=1, source_target_pairs={{0,8},{24,16},{1,9},{25,17},{2,10},{26,18},{3,11},{27,19},{4,12},{... | collective-permute-start | bytes 1179656 | tf_op jit(solution)/shard_map/ppermute | solution.py:281
  27.2 0.1 add_convert_fusion.spot_ref
  27.3 8.8 %collective-permute-done.1.piece_theirs_ref = bf16[384,512]{1,0:T(8,128)(2,1)S(1)} collective-permute-done((bf16[384,512]{1,0:T(8,128)(2,1)S(1)}, bf16[384,512]{1,0:T(8,128)(2,1)S(1)}, u32[]{:S(2)}, u32[]{:S(2)}) %collective-permute-start.1) | collective-permute-done | bytes 393248 | tf_op jit(solution)/shard_map/ppermute | solution.py:281
  36.1 2.7 %folded_parts.3 = (bf16[384,512]{1,0:T(8,128)(2,1)}, bf16[384,512]{1,0:T(8,128)(2,1)S(1)}) custom-call(s32[2]{0:T(128)S(1)} %add_convert_fusion.spot_ref, bf16[384,768]{1,0:T(8,128)(2,1)S(1)} %copy-done.2, bf16[384,768]{1,0:T(8,128)(2,1)S(1)} %collective-permute-done.theirs_ref, bf16[384,512]{1,0:T(8,128)(2,1)S(1)} %bitcast.17, ...), custom_call_target="tpu_custom_call" | custom-call | tf_op jit(solution)/shard_map/folded_parts/pallas_call | solution.py:20
  38.8 0.0 copy-done.4
  38.8 0.0 copy-start.7
  38.8 0.7 copy-done.7
  39.5 2.0 %all-to-all-done = bf16[8,48,1536]{2,1,0:T(8,128)(2,1)} async-done(((bf16[8,48,1536]{2,1,0:T(8,128)(2,1)}), bf16[8,48,1536]{2,1,0:T(8,128)(2,1)}, u32[]{:S(2)}, u32[]{:S(2)}) %all-to-all-start) | async-done | bytes 1179680 | tf_op jit(solution)/shard_map/all_to_all | solution.py:48
  41.5 2.1 %fusion = (bf16[384,768]{1,0:T(8,128)(2,1)S(1)}, bf16[384,768]{1,0:T(8,128)(2,1)}) fusion(bf16[384,1536]{1,0:T(8,128)(2,1)} %bitcast.4), kind=kLoop, calls=%fused_computation.1 | loop fusion | bytes 2359296 | tf_op jit(solution)/shard_map/slice | solution.py:287
  43.7 3.2 %collective-permute-start.4 = (bf16[384,768]{1,0:T(8,128)(2,1)S(1)}, bf16[384,768]{1,0:T(8,128)(2,1)}, u32[]{:S(2)}, u32[]{:S(2)}) collective-permute-start(bf16[384,768]{1,0:T(8,128)(2,1)S(1)} %get-tuple-element.37.refs_1_.piece_ref), channel_id=1, source_target_pairs={{0,8},{24,16},{1,9},{25,17},{2,10},{26,18},{3,11},{27,19},{4,12},{... | collective-permute-start | bytes 1769480 | tf_op jit(solution)/shard_map/ppermute | solution.py:288
  46.9 1.4 %collective-permute-start.3 = (bf16[384,512]{1,0:T(8,128)(2,1)}, bf16[384,512]{1,0:T(8,128)(2,1)}, u32[]{:S(2)}, u32[]{:S(2)}) collective-permute-start(bf16[384,512]{1,0:T(8,128)(2,1)} %get-tuple-element.32), channel_id=1, source_target_pairs={{8,16},{16,8},{9,17},{17,9},{10,18},{18,10},{11,19},{19,11},{12,20... | collective-permute-start | bytes 1179656 | tf_op jit(solution)/shard_map/ppermute | solution.py:291
  48.3 3.4 %collective-permute-start.2 = (bf16[384,768]{1,0:T(8,128)(2,1)}, bf16[384,768]{1,0:T(8,128)(2,1)}, u32[]{:S(2)}, u32[]{:S(2)}) collective-permute-start(bf16[384,768]{1,0:T(8,128)(2,1)} %get-tuple-element.38.piece_ref.refs_2_), channel_id=1, source_target_pairs={{0,8},{24,16},{1,9},{25,17},{2,10},{26,18},{3,11},{27,19},{4,12},{... | collective-permute-start | bytes 1769480 | tf_op jit(solution)/shard_map/ppermute | solution.py:288
  51.7 3.9 %all-to-all-start.2 = ((bf16[8,48,2048]{2,1,0:T(8,128)(2,1)}), bf16[8,48,2048]{2,1,0:T(8,128)(2,1)S(1)}, u32[]{:S(2)}, u32[]{:S(2)}) async-start(bf16[8,48,2048]{2,1,0:T(8,128)(2,1)} %bitcast.15), calls=%async_computation.2 | async-start | bytes 3145728 | tf_op jit(solution)/shard_map/all_to_all | solution.py:48
  55.5 0.0 collective-permute-done.3.got_ref
  55.5 4.3 %collective-permute-done.4.piece_theirs_ref = bf16[384,768]{1,0:T(8,128)(2,1)} collective-permute-done((bf16[384,768]{1,0:T(8,128)(2,1)S(1)}, bf16[384,768]{1,0:T(8,128)(2,1)}, u32[]{:S(2)}, u32[]{:S(2)}) %collective-permute-start.4) | collective-permute-done | bytes 589856 | tf_op jit(solution)/shard_map/ppermute | solution.py:288
  59.8 3.2 %folded_parts.5 = (bf16[384,768]{1,0:T(8,128)(2,1)S(1)}, bf16[384,768]{1,0:T(8,128)(2,1)S(1)}) custom-call(s32[2]{0:T(128)S(1)} %add_convert_fusion.spot_ref, bf16[384,768]{1,0:T(8,128)(2,1)S(1)} %copy-done.2, bf16[384,768]{1,0:T(8,128)(2,1)S(1)} %collective-permute-done.theirs_ref, bf16[384,768]{1,0:T(8,128)(2,1)S(1)} %get-tuple-element.37.refs_1_.piece_ref, ...), custom_call_target="tpu_custom_call" | custom-call | tf_op jit(solution)/shard_map/folded_parts/pallas_call | solution.py:20
  63.0 0.0 copy-start.8
  63.0 0.8 collective-permute-start.5
  63.9 7.3 %collective-permute-done.2.piece_theirs_ref = bf16[384,768]{1,0:T(8,128)(2,1)} collective-permute-done((bf16[384,768]{1,0:T(8,128)(2,1)}, bf16[384,768]{1,0:T(8,128)(2,1)}, u32[]{:S(2)}, u32[]{:S(2)}) %collective-permute-start.2) | collective-permute-done | bytes 589856 | tf_op jit(solution)/shard_map/ppermute | solution.py:288
  71.2 3.6 %folded_parts.4 = (bf16[384,768]{1,0:T(8,128)(2,1)S(1)}, bf16[384,768]{1,0:T(8,128)(2,1)S(1)}) custom-call(s32[2]{0:T(128)S(1)} %add_convert_fusion.spot_ref, bf16[384,768]{1,0:T(8,128)(2,1)S(1)} %copy-done.2, bf16[384,768]{1,0:T(8,128)(2,1)S(1)} %collective-permute-done.theirs_ref, bf16[384,768]{1,0:T(8,128)(2,1)} %get-tuple-element.38.piece_ref.refs_2_, ...), custom_call_target="tpu_custom_call" | custom-call | tf_op jit(solution)/shard_map/folded_parts/pallas_call | solution.py:20
  74.8 0.0 copy-start.5
  74.8 0.8 collective-permute-start.6
  75.6 0.0 collective-permute-done.5.got_ref
  75.7 0.7 finish.4
  76.4 1.3 %collective-permute-start.8 = (bf16[192,768]{1,0:T(8,128)(2,1)S(1)}, bf16[192,768]{1,0:T(8,128)(2,1)S(1)}, u32[]{:S(2)}, u32[]{:S(2)}) collective-permute-start(bf16[192,768]{1,0:T(8,128)(2,1)S(1)} %get-tuple-element.51), channel_id=1, source_target_pairs={{8,0},{16,24},{9,1},{17,25},{10,2},{18,26},{11,3},{19,27},{12,4},{... | collective-permute-start | bytes 884744 | tf_op jit(solution)/shard_map/ppermute | solution.py:307
  77.7 0.0 copy-done.8
  77.7 1.1 %finish.3 = (bf16[192,512]{1,0:T(8,128)(2,1)S(1)}, bf16[192,512]{1,0:T(8,128)(2,1)S(1)}) custom-call(s32[2]{0:T(128)S(1)} %add_convert_fusion.spot_ref, bf16[384,512]{1,0:T(8,128)(2,1)S(1)} %copy-done.8, bf16[384,512]{1,0:T(8,128)(2,1)} %collective-permute-done.3.got_ref), custom_call_target="tpu_custom_call" | custom-call | tf_op jit(solution)/shard_map/finish/pallas_call | solution.py:20
  78.8 0.0 copy-start.12
  78.8 0.0 copy-start.14
  78.9 1.3 %collective-permute-start.7 = (bf16[192,512]{1,0:T(8,128)(2,1)S(1)}, bf16[192,512]{1,0:T(8,128)(2,1)S(1)}, u32[]{:S(2)}, u32[]{:S(2)}) collective-permute-start(bf16[192,512]{1,0:T(8,128)(2,1)S(1)} %get-tuple-element.49), channel_id=1, source_target_pairs={{8,0},{16,24},{9,1},{17,25},{10,2},{18,26},{11,3},{19,27},{12,4},{... | collective-permute-start | bytes 589832 | tf_op jit(solution)/shard_map/ppermute | solution.py:307
  80.2 0.0 copy-done.1
  80.2 0.0 copy-done.5
  80.2 3.3 %grad_rows.1 = bf16[384,768]{1,0:T(8,128)(2,1)} custom-call(bf16[768,2048]{1,0:T(8,128)(2,1)S(1)} %bitcast.13, bf16[384,512]{1,0:T(8,128)(2,1)S(1)} %bitcast.18, bf16[384,768]{1,0:T(8,128)(2,1)S(1)} %get-tuple-element.37.refs_1_.piece_ref, bf16[384,768]{1,0:T(8,128)(2,1)} %get-tuple-element.38.piece_ref.refs_2_), custom_call_target="tpu_custom_call" | custom-call | tf_op jit(solution)/shard_map/grad_rows/pallas_call | solution.py:20
  83.5 0.0 collective-permute-done.6.got_ref
  83.5 9.3 %collective-permute-done.7.refs_3_ = bf16[192,512]{1,0:T(8,128)(2,1)S(1)} collective-permute-done((bf16[192,512]{1,0:T(8,128)(2,1)S(1)}, bf16[192,512]{1,0:T(8,128)(2,1)S(1)}, u32[]{:S(2)}, u32[]{:S(2)}) %collective-permute-start.7) | collective-permute-done | bytes 196640 | tf_op jit(solution)/shard_map/ppermute | solution.py:307
  92.8 0.0 collective-permute-done.8.refs_4_
  92.8 0.7 finish.5
  93.5 0.0 copy-done.9
  93.6 0.0 copy-start.10
  93.6 1.4 %collective-permute-start.9 = (bf16[192,768]{1,0:T(8,128)(2,1)S(1)}, bf16[192,768]{1,0:T(8,128)(2,1)S(1)}, u32[]{:S(2)}, u32[]{:S(2)}) collective-permute-start(bf16[192,768]{1,0:T(8,128)(2,1)S(1)} %get-tuple-element.54), channel_id=1, source_target_pairs={{8,0},{16,24},{9,1},{17,25},{10,2},{18,26},{11,3},{19,27},{12,4},{... | collective-permute-start | bytes 884744 | tf_op jit(solution)/shard_map/ppermute | solution.py:307
  95.0 0.0 all-to-all-done.2
  95.0 0.0 copy-done.12
  95.0 0.0 copy-done.14
  95.0 1.7 %combine.1 = bf16[128,2048]{1,0:T(8,128)(2,1)} custom-call(s32[2,128]{1,0:T(2,128)S(1)} %bitcast.20, f32[2,128]{1,0:T(2,128)S(1)} %bitcast.22, bf16[384,2048]{1,0:T(8,128)(2,1)S(1)} %bitcast.14), custom_call_target="tpu_custom_call" | custom-call | tf_op jit(solution)/shard_map/combine/pallas_call | solution.py:20
  96.8 5.6 %collective-permute-done.9.refs_5_ = bf16[192,768]{1,0:T(8,128)(2,1)S(1)} collective-permute-done((bf16[192,768]{1,0:T(8,128)(2,1)S(1)}, bf16[192,768]{1,0:T(8,128)(2,1)S(1)}, u32[]{:S(2)}, u32[]{:S(2)}) %collective-permute-start.9) | collective-permute-done | bytes 294944 | tf_op jit(solution)/shard_map/ppermute | solution.py:307
  102.4 0.0 copy-done.10
  102.4 1.5 %shares.1 = bf16[192,2048]{1,0:T(8,128)(2,1)} custom-call(s32[2]{0:T(128)S(1)} %add_convert_fusion.spot_ref, bf16[192,512]{1,0:T(8,128)(2,1)S(1)} %get-tuple-element.43.refs_0_, bf16[192,768]{1,0:T(8,128)(2,1)S(1)} %get-tuple-element.46.refs_1_, bf16[192,768]{1,0:T(8,128)(2,1)S(1)} %get-tuple-element.53.refs_2_, bf16[192,512]{1,0:T(8,128)(2,1)S(1)} %copy-done.10, ...), custom_call_target="tpu_custom_call" | custom-call | tf_op jit(solution)/shard_map/shares/pallas_call | solution.py:20
  (5 shorter events, 0.0 us)
Async XLA Ops:
  0.6 13.3 %copy-start.2 = (bf16[384,768]{1,0:T(8,128)(2,1)S(1)}, bf16[384,768]{1,0:T(8,128)(2,1)}, u32[]{:S(2)}) copy-start(bf16[384,768]{1,0:T(8,128)(2,1)} %mine_ref.5) | copy-start | bytes 1769476
  0.6 18.5 %collective-permute-start = (bf16[384,768]{1,0:T(8,128)(2,1)}, bf16[384,768]{1,0:T(8,128)(2,1)S(1)}, u32[]{:S(2)}, u32[]{:S(2)}) collective-permute-start(bf16[384,768]{1,0:T(8,128)(2,1)} %mine_ref.5), channel_id=1, source_target_pairs={{0,8},{24,16},{1,9},{25,17},{2,10},{26,18},{3,11},{27,19},{4,12},{... | collective-permute-start | bytes 1769480 | tf_op jit(solution)/shard_map/ppermute | solution.py:263
  5.7 1.0 %copy-start.6 = (bf16[128,2048]{1,0:T(8,128)(2,1)S(1)}, bf16[128,2048]{1,0:T(8,128)(2,1)}, u32[]{:S(2)}) copy-start(bf16[128,2048]{1,0:T(8,128)(2,1)} %grads_hbm.1) | copy-start | bytes 1572868
  6.8 0.7 copy-start.11
  7.5 0.7 copy-start.13
  10.1 11.2 %all-to-all-start.1 = ((bf16[8,48,512]{2,1,0:T(8,128)(2,1)}), bf16[8,48,512]{2,1,0:T(8,128)(2,1)S(1)}, u32[]{:S(2)}, u32[]{:S(2)}) async-start(bf16[8,48,512]{2,1,0:T(8,128)(2,1)} %bitcast.7), calls=%async_computation.1 | async-start | bytes 786432 | tf_op jit(solution)/shard_map/all_to_all | solution.py:48
  13.9 1.9 %copy-start = (bf16[1,768,2048]{2,1,0:T(8,128)(2,1)S(1)}, bf16[1,768,2048]{2,1,0:T(8,128)(2,1)}, u32[]{:S(2)}) copy-start(bf16[1,768,2048]{2,1,0:T(8,128)(2,1)} %param.9) | copy-start | bytes 9437188
  17.9 1.2 %copy-start.3 = (bf16[384,2048]{1,0:T(8,128)(2,1)}, bf16[384,2048]{1,0:T(8,128)(2,1)S(1)}, u32[]{:S(2)}) copy-start(bf16[384,2048]{1,0:T(8,128)(2,1)S(1)} %expert_rows.1) | copy-start | bytes 4718596
  21.3 17.5 %copy-start.4 = (bf16[8,48,512]{2,1,0:T(8,128)(2,1)}, bf16[8,48,512]{2,1,0:T(8,128)(2,1)S(1)}, u32[]{:S(2)}) copy-start(bf16[8,48,512]{2,1,0:T(8,128)(2,1)S(1)} %all-to-all-done.1) | copy-start | bytes 1179652
  21.3 20.2 %all-to-all-start = ((bf16[8,48,1536]{2,1,0:T(8,128)(2,1)}), bf16[8,48,1536]{2,1,0:T(8,128)(2,1)}, u32[]{:S(2)}, u32[]{:S(2)}) async-start(bf16[8,48,1536]{2,1,0:T(8,128)(2,1)} %bitcast.3), calls=%async_computation | async-start | bytes 2359296 | tf_op jit(solution)/shard_map/all_to_all | solution.py:48
  25.6 10.5 %collective-permute-start.1 = (bf16[384,512]{1,0:T(8,128)(2,1)S(1)}, bf16[384,512]{1,0:T(8,128)(2,1)S(1)}, u32[]{:S(2)}, u32[]{:S(2)}) collective-permute-start(bf16[384,512]{1,0:T(8,128)(2,1)S(1)} %bitcast.16), channel_id=1, source_target_pairs={{0,8},{24,16},{1,9},{25,17},{2,10},{26,18},{3,11},{27,19},{4,12},{... | collective-permute-start | bytes 1179656 | tf_op jit(solution)/shard_map/ppermute | solution.py:281
  38.8 0.8 copy-start.7
  43.7 16.1 %collective-permute-start.4 = (bf16[384,768]{1,0:T(8,128)(2,1)S(1)}, bf16[384,768]{1,0:T(8,128)(2,1)}, u32[]{:S(2)}, u32[]{:S(2)}) collective-permute-start(bf16[384,768]{1,0:T(8,128)(2,1)S(1)} %get-tuple-element.37.refs_1_.piece_ref), channel_id=1, source_target_pairs={{0,8},{24,16},{1,9},{25,17},{2,10},{26,18},{3,11},{27,19},{4,12},{... | collective-permute-start | bytes 1769480 | tf_op jit(solution)/shard_map/ppermute | solution.py:288
  46.9 8.7 %collective-permute-start.3 = (bf16[384,512]{1,0:T(8,128)(2,1)}, bf16[384,512]{1,0:T(8,128)(2,1)}, u32[]{:S(2)}, u32[]{:S(2)}) collective-permute-start(bf16[384,512]{1,0:T(8,128)(2,1)} %get-tuple-element.32), channel_id=1, source_target_pairs={{8,16},{16,8},{9,17},{17,9},{10,18},{18,10},{11,19},{19,11},{12,20... | collective-permute-start | bytes 1179656 | tf_op jit(solution)/shard_map/ppermute | solution.py:291
  48.3 22.9 %collective-permute-start.2 = (bf16[384,768]{1,0:T(8,128)(2,1)}, bf16[384,768]{1,0:T(8,128)(2,1)}, u32[]{:S(2)}, u32[]{:S(2)}) collective-permute-start(bf16[384,768]{1,0:T(8,128)(2,1)} %get-tuple-element.38.piece_ref.refs_2_), channel_id=1, source_target_pairs={{0,8},{24,16},{1,9},{25,17},{2,10},{26,18},{3,11},{27,19},{4,12},{... | collective-permute-start | bytes 1769480 | tf_op jit(solution)/shard_map/ppermute | solution.py:288
  51.7 43.3 %all-to-all-start.2 = ((bf16[8,48,2048]{2,1,0:T(8,128)(2,1)}), bf16[8,48,2048]{2,1,0:T(8,128)(2,1)S(1)}, u32[]{:S(2)}, u32[]{:S(2)}) async-start(bf16[8,48,2048]{2,1,0:T(8,128)(2,1)} %bitcast.15), calls=%async_computation.2 | async-start | bytes 3145728 | tf_op jit(solution)/shard_map/all_to_all | solution.py:48
  63.0 14.6 %copy-start.8 = (bf16[384,512]{1,0:T(8,128)(2,1)S(1)}, bf16[384,512]{1,0:T(8,128)(2,1)}, u32[]{:S(2)}) copy-start(bf16[384,512]{1,0:T(8,128)(2,1)} %copy-done.7) | copy-start | bytes 1179652
  63.0 12.6 %collective-permute-start.5 = (bf16[384,768]{1,0:T(8,128)(2,1)S(1)}, bf16[384,768]{1,0:T(8,128)(2,1)S(1)}, u32[]{:S(2)}, u32[]{:S(2)}) collective-permute-start(bf16[384,768]{1,0:T(8,128)(2,1)S(1)} %get-tuple-element.41), channel_id=1, source_target_pairs={{8,16},{16,8},{9,17},{17,9},{10,18},{18,10},{11,19},{19,11},{12,20... | collective-permute-start | bytes 1769480 | tf_op jit(solution)/shard_map/ppermute | solution.py:298
  71.2 8.9 %copy-start.1 = (bf16[1,768,2048]{2,1,0:T(8,128)(2,1)S(1)}, bf16[1,768,2048]{2,1,0:T(8,128)(2,1)}, u32[]{:S(2)}) copy-start(bf16[1,768,2048]{2,1,0:T(8,128)(2,1)} %param.9) | copy-start | bytes 9437188
  74.8 5.4 %copy-start.5 = (bf16[8,48,512]{2,1,0:T(8,128)(2,1)S(1)}, bf16[8,48,512]{2,1,0:T(8,128)(2,1)}, u32[]{:S(2)}) copy-start(bf16[8,48,512]{2,1,0:T(8,128)(2,1)} %copy-done.4) | copy-start | bytes 1179652
  74.8 8.7 %collective-permute-start.6 = (bf16[384,768]{1,0:T(8,128)(2,1)S(1)}, bf16[384,768]{1,0:T(8,128)(2,1)S(1)}, u32[]{:S(2)}, u32[]{:S(2)}) collective-permute-start(bf16[384,768]{1,0:T(8,128)(2,1)S(1)} %get-tuple-element.35), channel_id=1, source_target_pairs={{8,16},{16,8},{9,17},{17,9},{10,18},{18,10},{11,19},{19,11},{12,20... | collective-permute-start | bytes 1769480 | tf_op jit(solution)/shard_map/ppermute | solution.py:298
  76.4 16.4 %collective-permute-start.8 = (bf16[192,768]{1,0:T(8,128)(2,1)S(1)}, bf16[192,768]{1,0:T(8,128)(2,1)S(1)}, u32[]{:S(2)}, u32[]{:S(2)}) collective-permute-start(bf16[192,768]{1,0:T(8,128)(2,1)S(1)} %get-tuple-element.51), channel_id=1, source_target_pairs={{8,0},{16,24},{9,1},{17,25},{10,2},{18,26},{11,3},{19,27},{12,4},{... | collective-permute-start | bytes 884744 | tf_op jit(solution)/shard_map/ppermute | solution.py:307
  78.8 16.2 %copy-start.12 = (s32[128,2]{0,1:T(2,128)S(1)}, s32[128,2]{0,1:T(2,128)}, u32[]{:S(2)}) copy-start(s32[128,2]{0,1:T(2,128)} %param.7) | copy-start | bytes 3076
  78.8 16.2 %copy-start.14 = (f32[128,2]{0,1:T(2,128)S(1)}, f32[128,2]{0,1:T(2,128)}, u32[]{:S(2)}) copy-start(f32[128,2]{0,1:T(2,128)} %param.8) | copy-start | bytes 3076
  78.9 14.0 %collective-permute-start.7 = (bf16[192,512]{1,0:T(8,128)(2,1)S(1)}, bf16[192,512]{1,0:T(8,128)(2,1)S(1)}, u32[]{:S(2)}, u32[]{:S(2)}) collective-permute-start(bf16[192,512]{1,0:T(8,128)(2,1)S(1)} %get-tuple-element.49), channel_id=1, source_target_pairs={{8,0},{16,24},{9,1},{17,25},{10,2},{18,26},{11,3},{19,27},{12,4},{... | collective-permute-start | bytes 589832 | tf_op jit(solution)/shard_map/ppermute | solution.py:307
  92.8 0.7 copy-start.9
  93.6 8.8 %copy-start.10 = (bf16[192,512]{1,0:T(8,128)(2,1)S(1)}, bf16[192,512]{1,0:T(8,128)(2,1)}, u32[]{:S(2)}) copy-start(bf16[192,512]{1,0:T(8,128)(2,1)} %copy-done.9) | copy-start | bytes 589828
  93.6 8.8 %collective-permute-start.9 = (bf16[192,768]{1,0:T(8,128)(2,1)S(1)}, bf16[192,768]{1,0:T(8,128)(2,1)S(1)}, u32[]{:S(2)}, u32[]{:S(2)}) collective-permute-start(bf16[192,768]{1,0:T(8,128)(2,1)S(1)} %get-tuple-element.54), channel_id=1, source_target_pairs={{8,0},{16,24},{9,1},{17,25},{10,2},{18,26},{11,3},{19,27},{12,4},{... | collective-permute-start | bytes 884744 | tf_op jit(solution)/shard_map/ppermute | solution.py:307

commit v3 on v2

--- a/solution.py
+++ b/solution.py
@@ -6,13 +6,13 @@
 from jax.sharding import PartitionSpec as P
 
 grad_scale = 0.015625
-PARTS = ((4,), (6, 6))
+PARTS = ((5,), (6, 5))
 F32 = jnp.float32
 BF16 = jnp.bfloat16
 GROUP = ("ctx", "tp")
 
 
-def call(body, outs, ins, name, flops=0, smem=0, scratch=(), in_hbm=(), out_hbm=()):
+def call(body, outs, ins, name, flops=0, smem=0, scratch=(), in_hbm=(), out_hbm=(), limit=14):
     in_specs = [
         pl.BlockSpec(memory_space=pltpu.SMEM if i < smem else pltpu.HBM if i in in_hbm else pltpu.VMEM)
         for i in range(len(ins))
@@ -27,7 +27,7 @@
         scratch_shapes=scratch,
         name=name,
         cost_estimate=pl.CostEstimate(flops=0, bytes_accessed=0, transcendentals=0),
-        compiler_params=pltpu.CompilerParams(vmem_limit_bytes=14 * 2**20),
+        compiler_params=pltpu.CompilerParams(vmem_limit_bytes=limit * 2**20),
     )(*ins)
 
 
@@ -99,6 +99,7 @@
         "dispatch",
         2 * rows * tokens * sum(widths),
         in_hbm=(0, 1, 2),
+        limit=60,
         scratch=[
             pltpu.VMEM(ids.shape, ids.dtype),
             pltpu.VMEM(gates.shape, gates.dtype),
@@ -160,6 +161,7 @@
         "expert_rows",
         2 * rows.shape[0] * weight.size,
         out_hbm=(0,),
+        limit=60,
         scratch=[pltpu.VMEM(out.shape, out.dtype), pltpu.SemaphoreType.DMA((width // step,))],
     )[0]
 
@@ -191,33 +193,25 @@
     )[0]
 
 
-def folded_parts(spot, mine, theirs, piece, piece_theirs):
+def folded_part(spot, mine, theirs, piece, piece_theirs, stays):
     half, width = mine.shape[1] // 2, piece.shape[1]
 
-    def body(spot_ref, mine_ref, theirs_ref, piece_ref, piece_theirs_ref, give_ref, keep_hbm, keep_ref, sem):
-        def rows(which):
-            columns = pl.ds(pl.multiple_of(which * half, half), half)
-            return sum(
-                lax.dot_general(h[:, columns], p[...], (((0,), (0,)), ((), ())), preferred_element_type=F32)
-                for h, p in ((mine_ref, piece_ref), (theirs_ref, piece_theirs_ref))
-            )
-
-        keep_ref[...] = rows(spot_ref[0]).astype(BF16)
-        copy = pltpu.make_async_copy(keep_ref, keep_hbm, sem)
-        copy.start()
-        give_ref[...] = rows(1 - spot_ref[0]).astype(BF16)
-        copy.wait()
-
-    return call(
-        body,
-        [like((half, width))] * 2,
+    def body(spot_ref, mine_ref, theirs_ref, piece_ref, piece_theirs_ref, out_ref):
+        which = spot_ref[0] if stays else 1 - spot_ref[0]
+        columns = pl.ds(pl.multiple_of(which * half, half), half)
+        out_ref[...] = sum(
+            lax.dot_general(h[:, columns], p[...], (((0,), (0,)), ((), ())), preferred_element_type=F32)
+            for h, p in ((mine_ref, piece_ref), (theirs_ref, piece_theirs_ref))
+        ).astype(BF16)
+
+    return call(
+        body,
+        [like((half, width))],
         [spot, mine, theirs, piece, piece_theirs],
-        "folded_parts",
-        8 * mine.shape[0] * half * width,
+        "kept_part" if stays else "given_part",
+        4 * mine.shape[0] * half * width,
         smem=1,
-        out_hbm=(1,),
-        scratch=[pltpu.VMEM((half, width), BF16), pltpu.SemaphoreType.DMA],
-    )
+    )[0]
 
 
 def finish(spot, keep, got):
@@ -279,8 +273,8 @@
 
     first = exchange(outgoing[0], experts)
     pieces, folded = [first], [lax.ppermute(first, "dp", fold)]
-    give, keep = folded_parts(spot, hidden, theirs, pieces[0], folded[0])
-    gives, keeps = [give], [keep]
+    give = folded_part(spot, hidden, theirs, pieces[0], folded[0], False)
+    gives = [give]
     arrived = after(exchange(after(outgoing[1], expert_out, theirs), experts), give)
     start = 0
     for cut in widths[1]:
@@ -291,22 +285,29 @@
     got = [lax.ppermute(give, "dp", swap)]
     returned = exchange(after(expert_out, pieces[-1], give), experts)
     folded[1] = after(folded[1], got[0])
-    for i in range(1, last + 1):
-        give, keep = folded_parts(spot, hidden, theirs, pieces[i], folded[i])
+    for i in range(1, last):
+        give = folded_part(spot, hidden, theirs, pieces[i], folded[i], False)
         gives.append(give)
-        keeps.append(keep)
         got.append(lax.ppermute(give, "dp", swap))
 
-    got[:last] = after(tuple(got[:last]), gives[-1])
-    grad_hidden = grad_rows(list(after(tuple(pieces), gives[-1])), weight)
-    got[-1] = after(got[-1], grad_hidden)
+    early = list(after(tuple(pieces), gives[-1]))
+    grad_hidden = grad_rows(early, weight)
+    keeps = [folded_part(spot, hidden, theirs, early[0], folded[0], True)]
+    folded[last] = after(folded[last], grad_hidden, keeps[0])
+    give = folded_part(spot, hidden, theirs, pieces[last], folded[last], False)
+    gives.append(give)
+    got.append(lax.ppermute(give, "dp", swap))
+
+    late = after(tuple(pieces), give)
+    got[:last] = after(tuple(got[:last]), give)
+    keeps += [folded_part(spot, hidden, theirs, late[i], folded[i], True) for i in range(1, last + 1)]
     formed, handed = [], []
     for i in range(last + 1):
         own, give = finish(spot, keeps[i], got[i])
         formed.append(own)
         handed.append(lax.ppermute(give, "dp", back))
         if i < last:
-            got[-1] = after(got[-1], handed[-1])
+            got[-1] = after(got[-1], handed[-1] if i < last - 1 else formed[-1])
     combined = combine(ids, gates, returned, experts, capacity)
     grad_down = shares(spot, formed, handed)
     return (combined, grad_hidden, grad_down[None])

time: 105 us -> 100 us (0.952)
  waiting for transfers between devices: 39.5 us -> 33.3 us
  Pallas kernels: 22.7 us -> 25.3 us
  local copies, waits for them, and re-layouts: 8.39 us -> 6.49 us
  starting transfers between devices: 32.2 us -> 33.5 us
    ppermute x2, waiting for transfers between devices: 11.6 us -> 5.05 us  [local(): folded.append(lax.ppermute(pieces[-1], 'dp', fold))]
    pallas_call x11 -> x14, Pallas kernels: 22.7 us -> 25.3 us  [call(): pl.pallas_call(body, out_shape=tuple(outs), in_specs=in_specs, out_specs=...]
    ppermute x1, waiting for transfers between devices: 8.79 us -> 11 us  [local(): pieces, folded = ([first], [lax.ppermute(first, 'dp', fold)])]
    all_to_all x3, waiting for transfers between devices: 4.22 us -> 2.06 us  [exchange(): lax.all_to_all(shaped, GROUP, split_axis=0, concat_axis=0, tiled=True)]
    ppermute x1, waiting for transfers between devices: 0.01 us -> 2.15 us  [local(): theirs = lax.ppermute(hidden, 'dp', fold) if line else hidden]
    unnamed x30 -> x22, local copies, waits for them, and re-layouts: 6.26 us -> 4.31 us
    ppermute x3, waiting for transfers between devices: 14.9 us -> 13 us  [local(): handed.append(lax.ppermute(give, 'dp', back))]
    ppermute x2, starting transfers between devices: 6.59 us -> 7.75 us  [local(): folded.append(lax.ppermute(pieces[-1], 'dp', fold))]
  transfers between devices with their start and end apart: 13 -> 13, of which waited for: 7 -> 7; matrix products, arithmetic and copies ran while one was open for 0% -> 1% of each run, Pallas kernels for 20% -> 24%
where the time goes in v3:
time: 100 us; the launch traced here: 99.6 us
  starting transfers between devices  33.5 us (34%)
  waiting for transfers between devices  33.3 us (33%)
  Pallas kernels  25.3 us (25%)
  local copies, waits for them, and re-layouts  6.49 us (6%)
    pallas_call x14, Pallas kernels, call(): pl.pallas_call(body, out_shape=tuple(outs), in_specs=in_specs, out_specs=...  25.3 us
    ppermute x3, waiting for transfers between devices, local(): handed.append(lax.ppermute(give, 'dp', back))  13 us
    all_to_all x3, starting transfers between devices, exchange(): lax.all_to_all(shaped, GROUP, split_axis=0, concat_axis=0, tiled=True)  11.6 us
    ppermute x1, waiting for transfers between devices, local(): pieces, folded = ([first], [lax.ppermute(first, 'dp', fold)])  11 us
    ppermute x2, starting transfers between devices, local(): folded.append(lax.ppermute(pieces[-1], 'dp', fold))  7.75 us
    ppermute x2, waiting for transfers between devices, local(): folded.append(lax.ppermute(pieces[-1], 'dp', fold))  5.05 us
    ppermute x1, starting transfers between devices, local(): theirs = lax.ppermute(hidden, 'dp', fold) if line else hidden  4.97 us
    unnamed x22, local copies, waits for them, and re-layouts  4.31 us
  transfers between devices with their start and end apart: 13, of which 7 were waited for; matrix products, arithmetic and copies ran while one was open for 1% of the time, Pallas kernels for 24%

profile of v3, /device:TPU:0, one launch (start us, length us, event | category | flops | bytes accessed | tf_op | source)
XLA Modules:
  0.0 99.6 jit_solution(7486998290941216114)
XLA Ops:
  0.6 5.0 %collective-permute-start = (bf16[384,768]{1,0:T(8,128)(2,1)}, bf16[384,768]{1,0:T(8,128)(2,1)S(1)}, u32[]{:S(2)}, u32[]{:S(2)}) collective-permute-start(bf16[384,768]{1,0:T(8,128)(2,1)} %mine_ref.11), channel_id=1, source_target_pairs={{0,8},{24,16},{1,9},{25,17},{2,10},{26,18},{3,11},{27,19},{4,12},{... | collective-permute-start | bytes 1769480 | tf_op jit(solution)/shard_map/ppermute | solution.py:257
  5.6 2.7 %dispatch.1 = (bf16[384,640]{1,0:T(8,128)(2,1)}, bf16[384,1408]{1,0:T(8,128)(2,1)}) custom-call(s32[2,128]{1,0:T(2,128)} %bitcast.18, f32[2,128]{1,0:T(2,128)} %bitcast.20, bf16[128,2048]{1,0:T(8,128)(2,1)} %grads_hbm.1), custom_call_target="tpu_custom_call" | custom-call | tf_op jit(solution)/shard_map/dispatch/pallas_call | solution.py:20
  8.3 3.7 %all-to-all-start.1 = ((bf16[8,48,640]{2,1,0:T(8,128)(2,1)}), bf16[8,48,640]{2,1,0:T(8,128)(2,1)S(1)}, u32[]{:S(2)}, u32[]{:S(2)}) async-start(bf16[8,48,640]{2,1,0:T(8,128)(2,1)} %bitcast.27), calls=%async_computation.1 | async-start | bytes 983040 | tf_op jit(solution)/shard_map/all_to_all | solution.py:48
  12.0 4.3 %expert_rows.1 = bf16[384,2048]{1,0:T(8,128)(2,1)} custom-call(bf16[384,768]{1,0:T(8,128)(2,1)} %mine_ref.11, bf16[768,2048]{1,0:T(8,128)(2,1)} %bitcast.12), custom_call_target="tpu_custom_call" | custom-call | tf_op jit(solution)/shard_map/expert_rows/pallas_call | solution.py:20
  16.3 0.0 copy-start
  16.3 2.1 %collective-permute-done.theirs_ref = bf16[384,768]{1,0:T(8,128)(2,1)S(1)} collective-permute-done((bf16[384,768]{1,0:T(8,128)(2,1)}, bf16[384,768]{1,0:T(8,128)(2,1)S(1)}, u32[]{:S(2)}, u32[]{:S(2)}) %collective-permute-start) | collective-permute-done | bytes 589856 | tf_op jit(solution)/shard_map/ppermute | solution.py:257
  18.5 2.1 %all-to-all-done.1 = bf16[8,48,640]{2,1,0:T(8,128)(2,1)S(1)} async-done(((bf16[8,48,640]{2,1,0:T(8,128)(2,1)}), bf16[8,48,640]{2,1,0:T(8,128)(2,1)S(1)}, u32[]{:S(2)}, u32[]{:S(2)}) %all-to-all-start.1) | async-done | bytes 491552 | tf_op jit(solution)/shard_map/all_to_all | solution.py:48
  20.5 3.6 %all-to-all-start = ((bf16[8,48,1408]{2,1,0:T(8,128)(2,1)}), bf16[8,48,1408]{2,1,0:T(8,128)(2,1)S(1)}, u32[]{:S(2)}, u32[]{:S(2)}) async-start(bf16[8,48,1408]{2,1,0:T(8,128)(2,1)} %bitcast.25), calls=%async_computation | async-start | bytes 2162688 | tf_op jit(solution)/shard_map/all_to_all | solution.py:48
  24.1 2.4 %collective-permute-start.1 = (bf16[384,640]{1,0:T(8,128)(2,1)S(1)}, bf16[384,640]{1,0:T(8,128)(2,1)S(1)}, u32[]{:S(2)}, u32[]{:S(2)}) collective-permute-start(bf16[384,640]{1,0:T(8,128)(2,1)S(1)} %bitcast.14), channel_id=1, source_target_pairs={{0,8},{24,16},{1,9},{25,17},{2,10},{26,18},{3,11},{27,19},{4,12},{... | collective-permute-start | bytes 1474568 | tf_op jit(solution)/shard_map/ppermute | solution.py:275
  26.5 0.1 add_convert_fusion.spot_ref
  26.6 11.0 %collective-permute-done.1.piece_theirs_ref = bf16[384,640]{1,0:T(8,128)(2,1)S(1)} collective-permute-done((bf16[384,640]{1,0:T(8,128)(2,1)S(1)}, bf16[384,640]{1,0:T(8,128)(2,1)S(1)}, u32[]{:S(2)}, u32[]{:S(2)}) %collective-permute-start.1) | collective-permute-done | bytes 491552 | tf_op jit(solution)/shard_map/ppermute | solution.py:275
  37.6 0.0 copy-done
  37.6 0.0 copy-start.2
  37.6 2.1 %given_part.3 = bf16[384,640]{1,0:T(8,128)(2,1)} custom-call(s32[2]{0:T(128)S(1)} %add_convert_fusion.spot_ref, bf16[384,768]{1,0:T(8,128)(2,1)S(1)} %copy-done, bf16[384,768]{1,0:T(8,128)(2,1)S(1)} %collective-permute-done.theirs_ref, bf16[384,640]{1,0:T(8,128)(2,1)S(1)} %bitcast.15, bf16[384,640]{1,0:T(8,128)(2,1)S(1)} %collective-permute-done.1.piece_theirs_ref), custom_call_target="tpu_custom_call" | custom-call | tf_op jit(solution)/shard_map/given_part/pallas_call | solution.py:20
  39.7 0.0 all-to-all-done
  39.7 0.0 copy-done.2
  39.7 0.0 copy-start.10
  39.7 1.0 %copy-done.10 = bf16[8,48,1408]{2,1,0:T(8,128)(2,1)} copy-done((bf16[8,48,1408]{2,1,0:T(8,128)(2,1)}, bf16[8,48,1408]{2,1,0:T(8,128)(2,1)S(1)}, u32[]{:S(2)}) %copy-start.10) | copy-done | bytes 1081368
  40.7 1.1 %slice.7.piece_ref.refs_1_ = bf16[384,768]{1,0:T(8,128)(2,1)S(1)} slice(bf16[384,1408]{1,0:T(8,128)(2,1)} %bitcast.23), slice={[0:384], [0:768]} | slice | bytes 1179648 | tf_op jit(solution)/shard_map/slice | solution.py:281
  41.8 4.4 %collective-permute-start.2 = (bf16[384,768]{1,0:T(8,128)(2,1)S(1)}, bf16[384,768]{1,0:T(8,128)(2,1)S(1)}, u32[]{:S(2)}, u32[]{:S(2)}) collective-permute-start(bf16[384,768]{1,0:T(8,128)(2,1)S(1)} %slice.7.piece_ref.refs_1_), channel_id=1, source_target_pairs={{0,8},{24,16},{1,9},{25,17},{2,10},{26,18},{3,11},{27,19},{4,12},{... | collective-permute-start | bytes 1769480 | tf_op jit(solution)/shard_map/ppermute | solution.py:282
  46.2 1.5 %collective-permute-start.3 = (bf16[384,640]{1,0:T(8,128)(2,1)}, bf16[384,640]{1,0:T(8,128)(2,1)}, u32[]{:S(2)}, u32[]{:S(2)}) collective-permute-start(bf16[384,640]{1,0:T(8,128)(2,1)} %given_part.3), channel_id=1, source_target_pairs={{8,16},{16,8},{9,17},{17,9},{10,18},{18,10},{11,19},{19,11},{12,20... | collective-permute-start | bytes 1474568 | tf_op jit(solution)/shard_map/ppermute | solution.py:285
  47.7 1.1 %slice.6.refs_2_.piece_ref = bf16[384,640]{1,0:T(8,128)(2,1)S(1)} slice(bf16[384,1408]{1,0:T(8,128)(2,1)} %bitcast.24), slice={[0:384], [768:1408]} | slice | bytes 983040 | tf_op jit(solution)/shard_map/slice | solution.py:281
  48.8 4.3 %all-to-all-start.2 = ((bf16[8,48,2048]{2,1,0:T(8,128)(2,1)}), bf16[8,48,2048]{2,1,0:T(8,128)(2,1)}, u32[]{:S(2)}, u32[]{:S(2)}) async-start(bf16[8,48,2048]{2,1,0:T(8,128)(2,1)} %bitcast.22), calls=%async_computation.2 | async-start | bytes 3145728 | tf_op jit(solution)/shard_map/all_to_all | solution.py:48
  53.1 3.3 %collective-permute-start.5 = (bf16[384,640]{1,0:T(8,128)(2,1)S(1)}, bf16[384,640]{1,0:T(8,128)(2,1)S(1)}, u32[]{:S(2)}, u32[]{:S(2)}) collective-permute-start(bf16[384,640]{1,0:T(8,128)(2,1)S(1)} %slice.6.refs_2_.piece_ref), channel_id=1, source_target_pairs={{0,8},{24,16},{1,9},{25,17},{2,10},{26,18},{3,11},{27,19},{4,12},{... | collective-permute-start | bytes 1474568 | tf_op jit(solution)/shard_map/ppermute | solution.py:282
  56.4 0.0 collective-permute-done.3.got_ref
  56.5 3.5 %collective-permute-done.2.piece_theirs_ref = bf16[384,768]{1,0:T(8,128)(2,1)S(1)} collective-permute-done((bf16[384,768]{1,0:T(8,128)(2,1)S(1)}, bf16[384,768]{1,0:T(8,128)(2,1)S(1)}, u32[]{:S(2)}, u32[]{:S(2)}) %collective-permute-start.2) | collective-permute-done | bytes 589856 | tf_op jit(solution)/shard_map/ppermute | solution.py:282
  59.9 1.4 %given_part.4 = bf16[384,768]{1,0:T(8,128)(2,1)S(1)} custom-call(s32[2]{0:T(128)S(1)} %add_convert_fusion.spot_ref, bf16[384,768]{1,0:T(8,128)(2,1)S(1)} %copy-done, bf16[384,768]{1,0:T(8,128)(2,1)S(1)} %collective-permute-done.theirs_ref, bf16[384,768]{1,0:T(8,128)(2,1)S(1)} %slice.7.piece_ref.refs_1_, ...), custom_call_target="tpu_custom_call" | custom-call | tf_op jit(solution)/shard_map/given_part/pallas_call | solution.py:20
  61.3 0.7 collective-permute-start.4
  62.0 0.0 copy-start.1
  62.0 1.9 %copy-done.1 = bf16[1,768,2048]{2,1,0:T(8,128)(2,1)S(1)} copy-done((bf16[1,768,2048]{2,1,0:T(8,128)(2,1)S(1)}, bf16[1,768,2048]{2,1,0:T(8,128)(2,1)}, u32[]{:S(2)}) %copy-start.1) | copy-done | bytes 3145752
  63.9 0.0 copy-start.3
  63.9 2.4 %grad_rows.1 = bf16[384,768]{1,0:T(8,128)(2,1)} custom-call(bf16[768,2048]{1,0:T(8,128)(2,1)S(1)} %bitcast.13, bf16[384,640]{1,0:T(8,128)(2,1)S(1)} %bitcast.16, bf16[384,768]{1,0:T(8,128)(2,1)S(1)} %slice.7.piece_ref.refs_1_, bf16[384,640]{1,0:T(8,128)(2,1)S(1)} %slice.6.refs_2_.piece_ref), custom_call_target="tpu_custom_call" | custom-call | tf_op jit(solution)/shard_map/grad_rows/pallas_call | solution.py:20
  66.3 0.0 copy-done.3
  66.3 1.3 %kept_part.3.keep_ref = bf16[384,640]{1,0:T(8,128)(2,1)S(1)} custom-call(s32[2]{0:T(128)S(1)} %add_convert_fusion.spot_ref, bf16[384,768]{1,0:T(8,128)(2,1)S(1)} %copy-done, bf16[384,768]{1,0:T(8,128)(2,1)S(1)} %collective-permute-done.theirs_ref, bf16[384,640]{1,0:T(8,128)(2,1)S(1)} %bitcast.17, bf16[384,640]{1,0:T(8,128)(2,1)S(1)} %copy-done.3), custom_call_target="tpu_custom_call" | custom-call | tf_op jit(solution)/shard_map/kept_part/pallas_call | solution.py:20
  67.6 1.6 %collective-permute-done.5.piece_theirs_ref = bf16[384,640]{1,0:T(8,128)(2,1)S(1)} collective-permute-done((bf16[384,640]{1,0:T(8,128)(2,1)S(1)}, bf16[384,640]{1,0:T(8,128)(2,1)S(1)}, u32[]{:S(2)}, u32[]{:S(2)}) %collective-permute-start.5) | collective-permute-done | bytes 491552 | tf_op jit(solution)/shard_map/ppermute | solution.py:282
  69.2 1.3 %given_part.5 = bf16[384,640]{1,0:T(8,128)(2,1)S(1)} custom-call(s32[2]{0:T(128)S(1)} %add_convert_fusion.spot_ref, bf16[384,768]{1,0:T(8,128)(2,1)S(1)} %copy-done, bf16[384,768]{1,0:T(8,128)(2,1)S(1)} %collective-permute-done.theirs_ref, bf16[384,640]{1,0:T(8,128)(2,1)S(1)} %slice.6.refs_2_.piece_ref, ...), custom_call_target="tpu_custom_call" | custom-call | tf_op jit(solution)/shard_map/given_part/pallas_call | solution.py:20
  70.5 0.7 collective-permute-start.6
  71.2 0.0 collective-permute-done.4.got_ref
  71.2 1.2 %finish.3 = (bf16[192,640]{1,0:T(8,128)(2,1)S(1)}, bf16[192,640]{1,0:T(8,128)(2,1)S(1)}) custom-call(s32[2]{0:T(128)S(1)} %add_convert_fusion.spot_ref, bf16[384,640]{1,0:T(8,128)(2,1)S(1)} %kept_part.3.keep_ref, bf16[384,640]{1,0:T(8,128)(2,1)} %collective-permute-done.3.got_ref), custom_call_target="tpu_custom_call" | custom-call | tf_op jit(solution)/shard_map/finish/pallas_call | solution.py:20
  72.4 0.0 copy-start.4
  72.4 0.7 copy-done.4
  73.1 1.3 %collective-permute-start.7 = (bf16[192,640]{1,0:T(8,128)(2,1)S(1)}, bf16[192,640]{1,0:T(8,128)(2,1)S(1)}, u32[]{:S(2)}, u32[]{:S(2)}) collective-permute-start(bf16[192,640]{1,0:T(8,128)(2,1)S(1)} %get-tuple-element.41), channel_id=1, source_target_pairs={{8,0},{16,24},{9,1},{17,25},{10,2},{18,26},{11,3},{19,27},{12,4},{... | collective-permute-start | bytes 737288 | tf_op jit(solution)/shard_map/ppermute | solution.py:308
  74.4 1.3 %kept_part.4.keep_ref = bf16[384,768]{1,0:T(8,128)(2,1)S(1)} custom-call(s32[2]{0:T(128)S(1)} %add_convert_fusion.spot_ref, bf16[384,768]{1,0:T(8,128)(2,1)S(1)} %copy-done, bf16[384,768]{1,0:T(8,128)(2,1)S(1)} %collective-permute-done.theirs_ref, bf16[384,768]{1,0:T(8,128)(2,1)S(1)} %slice.7.piece_ref.refs_1_, ...), custom_call_target="tpu_custom_call" | custom-call | tf_op jit(solution)/shard_map/kept_part/pallas_call | solution.py:20
  75.7 0.7 finish.4
  76.5 0.0 copy-start.8
  76.5 0.0 copy-start.9
  76.5 1.3 %collective-permute-start.8 = (bf16[192,768]{1,0:T(8,128)(2,1)S(1)}, bf16[192,768]{1,0:T(8,128)(2,1)S(1)}, u32[]{:S(2)}, u32[]{:S(2)}) collective-permute-start(bf16[192,768]{1,0:T(8,128)(2,1)S(1)} %get-tuple-element.45), channel_id=1, source_target_pairs={{8,0},{16,24},{9,1},{17,25},{10,2},{18,26},{11,3},{19,27},{12,4},{... | collective-permute-start | bytes 884744 | tf_op jit(solution)/shard_map/ppermute | solution.py:308
  77.8 1.3 %kept_part.5.keep_ref = bf16[384,640]{1,0:T(8,128)(2,1)S(1)} custom-call(s32[2]{0:T(128)S(1)} %add_convert_fusion.spot_ref, bf16[384,768]{1,0:T(8,128)(2,1)S(1)} %copy-done, bf16[384,768]{1,0:T(8,128)(2,1)S(1)} %collective-permute-done.theirs_ref, bf16[384,640]{1,0:T(8,128)(2,1)S(1)} %slice.6.refs_2_.piece_ref, ...), custom_call_target="tpu_custom_call" | custom-call | tf_op jit(solution)/shard_map/kept_part/pallas_call | solution.py:20
  79.1 0.0 copy-start.5
  79.1 0.0 collective-permute-done.6.got_ref
  79.1 9.4 %collective-permute-done.7.refs_3_ = bf16[192,640]{1,0:T(8,128)(2,1)S(1)} collective-permute-done((bf16[192,640]{1,0:T(8,128)(2,1)S(1)}, bf16[192,640]{1,0:T(8,128)(2,1)S(1)}, u32[]{:S(2)}, u32[]{:S(2)}) %collective-permute-start.7) | collective-permute-done | bytes 245792 | tf_op jit(solution)/shard_map/ppermute | solution.py:308
  88.5 0.0 copy-start.6
  88.5 0.7 copy-done.6
  89.2 0.7 finish.5
  89.9 1.3 %collective-permute-start.9 = (bf16[192,640]{1,0:T(8,128)(2,1)S(1)}, bf16[192,640]{1,0:T(8,128)(2,1)S(1)}, u32[]{:S(2)}, u32[]{:S(2)}) collective-permute-start(bf16[192,640]{1,0:T(8,128)(2,1)S(1)} %get-tuple-element.46), channel_id=1, source_target_pairs={{8,0},{16,24},{9,1},{17,25},{10,2},{18,26},{11,3},{19,27},{12,4},{... | collective-permute-start | bytes 737288 | tf_op jit(solution)/shard_map/ppermute | solution.py:308
  91.2 0.0 all-to-all-done.2
  91.3 0.0 copy-done.8
  91.3 0.0 copy-done.9
  91.3 3.1 %combine.1 = bf16[128,2048]{1,0:T(8,128)(2,1)} custom-call(s32[2,128]{1,0:T(2,128)S(1)} %bitcast.19, f32[2,128]{1,0:T(2,128)S(1)} %bitcast.21, bf16[384,2048]{1,0:T(8,128)(2,1)} %bitcast.10.returned_ref), custom_call_target="tpu_custom_call" | custom-call | tf_op jit(solution)/shard_map/combine/pallas_call | solution.py:20
  94.4 0.0 collective-permute-done.8.refs_4_
  94.4 3.6 %collective-permute-done.9.refs_5_ = bf16[192,640]{1,0:T(8,128)(2,1)S(1)} collective-permute-done((bf16[192,640]{1,0:T(8,128)(2,1)S(1)}, bf16[192,640]{1,0:T(8,128)(2,1)S(1)}, u32[]{:S(2)}, u32[]{:S(2)}) %collective-permute-start.9) | collective-permute-done | bytes 245792 | tf_op jit(solution)/shard_map/ppermute | solution.py:308
  98.0 0.0 copy-done.5
  98.0 0.0 copy-done.7
  98.0 1.5 %shares.1 = bf16[192,2048]{1,0:T(8,128)(2,1)} custom-call(s32[2]{0:T(128)S(1)} %add_convert_fusion.spot_ref, bf16[192,640]{1,0:T(8,128)(2,1)S(1)} %copy-done.5, bf16[192,768]{1,0:T(8,128)(2,1)S(1)} %get-tuple-element.39.refs_1_, bf16[192,640]{1,0:T(8,128)(2,1)S(1)} %get-tuple-element.44.refs_2_, bf16[192,640]{1,0:T(8,128)(2,1)S(1)} %copy-done.7, ...), custom_call_target="tpu_custom_call" | custom-call | tf_op jit(solution)/shard_map/shares/pallas_call | solution.py:20
  (1 shorter events, 0.0 us)
Async XLA Ops:
  0.6 17.8 %collective-permute-start = (bf16[384,768]{1,0:T(8,128)(2,1)}, bf16[384,768]{1,0:T(8,128)(2,1)S(1)}, u32[]{:S(2)}, u32[]{:S(2)}) collective-permute-start(bf16[384,768]{1,0:T(8,128)(2,1)} %mine_ref.11), channel_id=1, source_target_pairs={{0,8},{24,16},{1,9},{25,17},{2,10},{26,18},{3,11},{27,19},{4,12},{... | collective-permute-start | bytes 1769480 | tf_op jit(solution)/shard_map/ppermute | solution.py:257
  8.3 12.2 %all-to-all-start.1 = ((bf16[8,48,640]{2,1,0:T(8,128)(2,1)}), bf16[8,48,640]{2,1,0:T(8,128)(2,1)S(1)}, u32[]{:S(2)}, u32[]{:S(2)}) async-start(bf16[8,48,640]{2,1,0:T(8,128)(2,1)} %bitcast.27), calls=%async_computation.1 | async-start | bytes 983040 | tf_op jit(solution)/shard_map/all_to_all | solution.py:48
  16.3 21.3 %copy-start = (bf16[384,768]{1,0:T(8,128)(2,1)S(1)}, bf16[384,768]{1,0:T(8,128)(2,1)}, u32[]{:S(2)}) copy-start(bf16[384,768]{1,0:T(8,128)(2,1)} %mine_ref.11) | copy-start | bytes 1769476
  20.5 19.2 %all-to-all-start = ((bf16[8,48,1408]{2,1,0:T(8,128)(2,1)}), bf16[8,48,1408]{2,1,0:T(8,128)(2,1)S(1)}, u32[]{:S(2)}, u32[]{:S(2)}) async-start(bf16[8,48,1408]{2,1,0:T(8,128)(2,1)} %bitcast.25), calls=%async_computation | async-start | bytes 2162688 | tf_op jit(solution)/shard_map/all_to_all | solution.py:48
  24.1 13.5 %collective-permute-start.1 = (bf16[384,640]{1,0:T(8,128)(2,1)S(1)}, bf16[384,640]{1,0:T(8,128)(2,1)S(1)}, u32[]{:S(2)}, u32[]{:S(2)}) collective-permute-start(bf16[384,640]{1,0:T(8,128)(2,1)S(1)} %bitcast.14), channel_id=1, source_target_pairs={{0,8},{24,16},{1,9},{25,17},{2,10},{26,18},{3,11},{27,19},{4,12},{... | collective-permute-start | bytes 1474568 | tf_op jit(solution)/shard_map/ppermute | solution.py:275
  37.6 2.1 %copy-start.2 = (bf16[384,640]{1,0:T(8,128)(2,1)}, bf16[384,640]{1,0:T(8,128)(2,1)S(1)}, u32[]{:S(2)}) copy-start(bf16[384,640]{1,0:T(8,128)(2,1)S(1)} %collective-permute-done.1.piece_theirs_ref) | copy-start | bytes 1474564
  39.7 1.0 %copy-start.10 = (bf16[8,48,1408]{2,1,0:T(8,128)(2,1)}, bf16[8,48,1408]{2,1,0:T(8,128)(2,1)S(1)}, u32[]{:S(2)}) copy-start(bf16[8,48,1408]{2,1,0:T(8,128)(2,1)S(1)} %all-to-all-done) | copy-start | bytes 3244036
  41.8 18.1 %collective-permute-start.2 = (bf16[384,768]{1,0:T(8,128)(2,1)S(1)}, bf16[384,768]{1,0:T(8,128)(2,1)S(1)}, u32[]{:S(2)}, u32[]{:S(2)}) collective-permute-start(bf16[384,768]{1,0:T(8,128)(2,1)S(1)} %slice.7.piece_ref.refs_1_), channel_id=1, source_target_pairs={{0,8},{24,16},{1,9},{25,17},{2,10},{26,18},{3,11},{27,19},{4,12},{... | collective-permute-start | bytes 1769480 | tf_op jit(solution)/shard_map/ppermute | solution.py:282
  46.2 10.2 %collective-permute-start.3 = (bf16[384,640]{1,0:T(8,128)(2,1)}, bf16[384,640]{1,0:T(8,128)(2,1)}, u32[]{:S(2)}, u32[]{:S(2)}) collective-permute-start(bf16[384,640]{1,0:T(8,128)(2,1)} %given_part.3), channel_id=1, source_target_pairs={{8,16},{16,8},{9,17},{17,9},{10,18},{18,10},{11,19},{19,11},{12,20... | collective-permute-start | bytes 1474568 | tf_op jit(solution)/shard_map/ppermute | solution.py:285
  48.8 42.5 %all-to-all-start.2 = ((bf16[8,48,2048]{2,1,0:T(8,128)(2,1)}), bf16[8,48,2048]{2,1,0:T(8,128)(2,1)}, u32[]{:S(2)}, u32[]{:S(2)}) async-start(bf16[8,48,2048]{2,1,0:T(8,128)(2,1)} %bitcast.22), calls=%async_computation.2 | async-start | bytes 3145728 | tf_op jit(solution)/shard_map/all_to_all | solution.py:48
  53.1 16.1 %collective-permute-start.5 = (bf16[384,640]{1,0:T(8,128)(2,1)S(1)}, bf16[384,640]{1,0:T(8,128)(2,1)S(1)}, u32[]{:S(2)}, u32[]{:S(2)}) collective-permute-start(bf16[384,640]{1,0:T(8,128)(2,1)S(1)} %slice.6.refs_2_.piece_ref), channel_id=1, source_target_pairs={{0,8},{24,16},{1,9},{25,17},{2,10},{26,18},{3,11},{27,19},{4,12},{... | collective-permute-start | bytes 1474568 | tf_op jit(solution)/shard_map/ppermute | solution.py:282
  61.3 9.9 %collective-permute-start.4 = (bf16[384,768]{1,0:T(8,128)(2,1)S(1)}, bf16[384,768]{1,0:T(8,128)(2,1)S(1)}, u32[]{:S(2)}, u32[]{:S(2)}) collective-permute-start(bf16[384,768]{1,0:T(8,128)(2,1)S(1)} %given_part.4), channel_id=1, source_target_pairs={{8,16},{16,8},{9,17},{17,9},{10,18},{18,10},{11,19},{19,11},{12,20... | collective-permute-start | bytes 1769480 | tf_op jit(solution)/shard_map/ppermute | solution.py:291
  62.0 1.9 %copy-start.1 = (bf16[1,768,2048]{2,1,0:T(8,128)(2,1)S(1)}, bf16[1,768,2048]{2,1,0:T(8,128)(2,1)}, u32[]{:S(2)}) copy-start(bf16[1,768,2048]{2,1,0:T(8,128)(2,1)} %param.9) | copy-start | bytes 9437188
  63.9 2.4 %copy-start.3 = (bf16[384,640]{1,0:T(8,128)(2,1)S(1)}, bf16[384,640]{1,0:T(8,128)(2,1)}, u32[]{:S(2)}) copy-start(bf16[384,640]{1,0:T(8,128)(2,1)} %copy-done.2) | copy-start | bytes 1474564
  70.5 8.6 %collective-permute-start.6 = (bf16[384,640]{1,0:T(8,128)(2,1)S(1)}, bf16[384,640]{1,0:T(8,128)(2,1)S(1)}, u32[]{:S(2)}, u32[]{:S(2)}) collective-permute-start(bf16[384,640]{1,0:T(8,128)(2,1)S(1)} %given_part.5), channel_id=1, source_target_pairs={{8,16},{16,8},{9,17},{17,9},{10,18},{18,10},{11,19},{19,11},{12,20... | collective-permute-start | bytes 1474568 | tf_op jit(solution)/shard_map/ppermute | solution.py:299
  72.4 0.7 copy-start.4
  73.1 15.4 %collective-permute-start.7 = (bf16[192,640]{1,0:T(8,128)(2,1)S(1)}, bf16[192,640]{1,0:T(8,128)(2,1)S(1)}, u32[]{:S(2)}, u32[]{:S(2)}) collective-permute-start(bf16[192,640]{1,0:T(8,128)(2,1)S(1)} %get-tuple-element.41), channel_id=1, source_target_pairs={{8,0},{16,24},{9,1},{17,25},{10,2},{18,26},{11,3},{19,27},{12,4},{... | collective-permute-start | bytes 737288 | tf_op jit(solution)/shard_map/ppermute | solution.py:308
  76.5 14.8 %copy-start.8 = (s32[128,2]{0,1:T(2,128)S(1)}, s32[128,2]{0,1:T(2,128)}, u32[]{:S(2)}) copy-start(s32[128,2]{0,1:T(2,128)} %param.7) | copy-start | bytes 3076
  76.5 14.8 %copy-start.9 = (f32[128,2]{0,1:T(2,128)S(1)}, f32[128,2]{0,1:T(2,128)}, u32[]{:S(2)}) copy-start(f32[128,2]{0,1:T(2,128)} %param.8) | copy-start | bytes 3076
  76.5 17.9 %collective-permute-start.8 = (bf16[192,768]{1,0:T(8,128)(2,1)S(1)}, bf16[192,768]{1,0:T(8,128)(2,1)S(1)}, u32[]{:S(2)}, u32[]{:S(2)}) collective-permute-start(bf16[192,768]{1,0:T(8,128)(2,1)S(1)} %get-tuple-element.45), channel_id=1, source_target_pairs={{8,0},{16,24},{9,1},{17,25},{10,2},{18,26},{11,3},{19,27},{12,4},{... | collective-permute-start | bytes 884744 | tf_op jit(solution)/shard_map/ppermute | solution.py:308
  79.1 18.9 %copy-start.5 = (bf16[192,640]{1,0:T(8,128)(2,1)S(1)}, bf16[192,640]{1,0:T(8,128)(2,1)}, u32[]{:S(2)}) copy-start(bf16[192,640]{1,0:T(8,128)(2,1)} %copy-done.4) | copy-start | bytes 737284
  88.5 0.7 copy-start.6
  89.2 8.8 %copy-start.7 = (bf16[192,640]{1,0:T(8,128)(2,1)S(1)}, bf16[192,640]{1,0:T(8,128)(2,1)}, u32[]{:S(2)}) copy-start(bf16[192,640]{1,0:T(8,128)(2,1)} %copy-done.6) | copy-start | bytes 737284
  89.9 8.1 %collective-permute-start.9 = (bf16[192,640]{1,0:T(8,128)(2,1)S(1)}, bf16[192,640]{1,0:T(8,128)(2,1)S(1)}, u32[]{:S(2)}, u32[]{:S(2)}) collective-permute-start(bf16[192,640]{1,0:T(8,128)(2,1)S(1)} %get-tuple-element.46), channel_id=1, source_target_pairs={{8,0},{16,24},{9,1},{17,25},{10,2},{18,26},{11,3},{19,27},{12,4},{... | collective-permute-start | bytes 737288 | tf_op jit(solution)/shard_map/ppermute | solution.py:308

commit v4 on v3

--- a/solution.py
+++ b/solution.py
@@ -307,7 +307,7 @@
         formed.append(own)
         handed.append(lax.ppermute(give, "dp", back))
         if i < last:
-            got[-1] = after(got[-1], handed[-1] if i < last - 1 else formed[-1])
+            got[-1] = after(got[-1], formed[-1])
     combined = combine(ids, gates, returned, experts, capacity)
     grad_down = shares(spot, formed, handed)
     return (combined, grad_hidden, grad_down[None])

time: 100 us -> 103 us (1.030)
  waiting for transfers between devices: 33.3 us -> 37.2 us
  local copies, waits for them, and re-layouts: 6.49 us -> 5.07 us
    ppermute x3, waiting for transfers between devices: 13 us -> 16.9 us  [local(): handed.append(lax.ppermute(give, 'dp', back))]
    unnamed x22 -> x14, local copies, waits for them, and re-layouts: 4.31 us -> 2.9 us
  transfers between devices with their start and end apart: 13 -> 13, of which waited for: 7 -> 7; matrix products, arithmetic and copies ran while one was open for 1% -> 1% of each run, Pallas kernels for 24% -> 23%
where the time goes in v4:
time: 103 us; the launch traced here: 102 us
  waiting for transfers between devices  37.2 us (36%)
  starting transfers between devices  33.5 us (33%)
  Pallas kernels  25.3 us (25%)
  local copies, waits for them, and re-layouts  5.07 us (5%)
    pallas_call x14, Pallas kernels, call(): pl.pallas_call(body, out_shape=tuple(outs), in_specs=in_specs, out_specs=...  25.3 us
    ppermute x3, waiting for transfers between devices, local(): handed.append(lax.ppermute(give, 'dp', back))  16.9 us
    all_to_all x3, starting transfers between devices, exchange(): lax.all_to_all(shaped, GROUP, split_axis=0, concat_axis=0, tiled=True)  11.6 us
    ppermute x1, waiting for transfers between devices, local(): pieces, folded = ([first], [lax.ppermute(first, 'dp', fold)])  11 us
    ppermute x2, starting transfers between devices, local(): folded.append(lax.ppermute(pieces[-1], 'dp', fold))  7.77 us
    ppermute x2, waiting for transfers between devices, local(): folded.append(lax.ppermute(pieces[-1], 'dp', fold))  5.07 us
    ppermute x1, starting transfers between devices, local(): theirs = lax.ppermute(hidden, 'dp', fold) if line else hidden  4.97 us
    ppermute x3, starting transfers between devices, local(): handed.append(lax.ppermute(give, 'dp', back))  3.88 us
  transfers between devices with their start and end apart: 13, of which 7 were waited for; matrix products, arithmetic and copies ran while one was open for 1% of the time, Pallas kernels for 23%

profile of v4, /device:TPU:0, one launch (start us, length us, event | category | flops | bytes accessed | tf_op | source)
XLA Modules:
  0.0 102.0 jit_solution(16262866844178192224)
XLA Ops:
  0.6 5.0 %collective-permute-start = (bf16[384,768]{1,0:T(8,128)(2,1)}, bf16[384,768]{1,0:T(8,128)(2,1)S(1)}, u32[]{:S(2)}, u32[]{:S(2)}) collective-permute-start(bf16[384,768]{1,0:T(8,128)(2,1)} %mine_ref.11), channel_id=1, source_target_pairs={{0,8},{24,16},{1,9},{25,17},{2,10},{26,18},{3,11},{27,19},{4,12},{... | collective-permute-start | bytes 1769480 | tf_op jit(solution)/shard_map/ppermute | solution.py:257
  5.6 2.6 %dispatch.1 = (bf16[384,640]{1,0:T(8,128)(2,1)}, bf16[384,1408]{1,0:T(8,128)(2,1)}) custom-call(s32[2,128]{1,0:T(2,128)} %bitcast.18, f32[2,128]{1,0:T(2,128)} %bitcast.20, bf16[128,2048]{1,0:T(8,128)(2,1)} %grads_hbm.1), custom_call_target="tpu_custom_call" | custom-call | tf_op jit(solution)/shard_map/dispatch/pallas_call | solution.py:20
  8.3 3.7 %all-to-all-start.1 = ((bf16[8,48,640]{2,1,0:T(8,128)(2,1)}), bf16[8,48,640]{2,1,0:T(8,128)(2,1)S(1)}, u32[]{:S(2)}, u32[]{:S(2)}) async-start(bf16[8,48,640]{2,1,0:T(8,128)(2,1)} %bitcast.27), calls=%async_computation.1 | async-start | bytes 983040 | tf_op jit(solution)/shard_map/all_to_all | solution.py:48
  12.0 4.3 %expert_rows.1 = bf16[384,2048]{1,0:T(8,128)(2,1)} custom-call(bf16[384,768]{1,0:T(8,128)(2,1)} %mine_ref.11, bf16[768,2048]{1,0:T(8,128)(2,1)} %bitcast.12), custom_call_target="tpu_custom_call" | custom-call | tf_op jit(solution)/shard_map/expert_rows/pallas_call | solution.py:20
  16.3 0.0 copy-start
  16.3 2.2 %collective-permute-done.theirs_ref = bf16[384,768]{1,0:T(8,128)(2,1)S(1)} collective-permute-done((bf16[384,768]{1,0:T(8,128)(2,1)}, bf16[384,768]{1,0:T(8,128)(2,1)S(1)}, u32[]{:S(2)}, u32[]{:S(2)}) %collective-permute-start) | collective-permute-done | bytes 589856 | tf_op jit(solution)/shard_map/ppermute | solution.py:257
  18.5 2.0 %all-to-all-done.1 = bf16[8,48,640]{2,1,0:T(8,128)(2,1)S(1)} async-done(((bf16[8,48,640]{2,1,0:T(8,128)(2,1)}), bf16[8,48,640]{2,1,0:T(8,128)(2,1)S(1)}, u32[]{:S(2)}, u32[]{:S(2)}) %all-to-all-start.1) | async-done | bytes 491552 | tf_op jit(solution)/shard_map/all_to_all | solution.py:48
  20.5 3.6 %all-to-all-start = ((bf16[8,48,1408]{2,1,0:T(8,128)(2,1)}), bf16[8,48,1408]{2,1,0:T(8,128)(2,1)S(1)}, u32[]{:S(2)}, u32[]{:S(2)}) async-start(bf16[8,48,1408]{2,1,0:T(8,128)(2,1)} %bitcast.25), calls=%async_computation | async-start | bytes 2162688 | tf_op jit(solution)/shard_map/all_to_all | solution.py:48
  24.1 2.4 %collective-permute-start.1 = (bf16[384,640]{1,0:T(8,128)(2,1)S(1)}, bf16[384,640]{1,0:T(8,128)(2,1)S(1)}, u32[]{:S(2)}, u32[]{:S(2)}) collective-permute-start(bf16[384,640]{1,0:T(8,128)(2,1)S(1)} %bitcast.14), channel_id=1, source_target_pairs={{0,8},{24,16},{1,9},{25,17},{2,10},{26,18},{3,11},{27,19},{4,12},{... | collective-permute-start | bytes 1474568 | tf_op jit(solution)/shard_map/ppermute | solution.py:275
  26.5 0.1 add_convert_fusion.spot_ref
  26.6 11.0 %collective-permute-done.1.piece_theirs_ref = bf16[384,640]{1,0:T(8,128)(2,1)S(1)} collective-permute-done((bf16[384,640]{1,0:T(8,128)(2,1)S(1)}, bf16[384,640]{1,0:T(8,128)(2,1)S(1)}, u32[]{:S(2)}, u32[]{:S(2)}) %collective-permute-start.1) | collective-permute-done | bytes 491552 | tf_op jit(solution)/shard_map/ppermute | solution.py:275
  37.6 0.0 copy-done
  37.6 0.0 copy-start.2
  37.6 2.1 %given_part.3 = bf16[384,640]{1,0:T(8,128)(2,1)} custom-call(s32[2]{0:T(128)S(1)} %add_convert_fusion.spot_ref, bf16[384,768]{1,0:T(8,128)(2,1)S(1)} %copy-done, bf16[384,768]{1,0:T(8,128)(2,1)S(1)} %collective-permute-done.theirs_ref, bf16[384,640]{1,0:T(8,128)(2,1)S(1)} %bitcast.15, bf16[384,640]{1,0:T(8,128)(2,1)S(1)} %collective-permute-done.1.piece_theirs_ref), custom_call_target="tpu_custom_call" | custom-call | tf_op jit(solution)/shard_map/given_part/pallas_call | solution.py:20
  39.7 0.0 all-to-all-done
  39.7 0.0 copy-done.2
  39.7 0.0 copy-start.6
  39.7 1.0 copy-done.6
  40.7 1.1 %slice.7.piece_ref.refs_1_ = bf16[384,768]{1,0:T(8,128)(2,1)S(1)} slice(bf16[384,1408]{1,0:T(8,128)(2,1)} %bitcast.23), slice={[0:384], [0:768]} | slice | bytes 1179648 | tf_op jit(solution)/shard_map/slice | solution.py:281
  41.8 4.4 %collective-permute-start.2 = (bf16[384,768]{1,0:T(8,128)(2,1)S(1)}, bf16[384,768]{1,0:T(8,128)(2,1)S(1)}, u32[]{:S(2)}, u32[]{:S(2)}) collective-permute-start(bf16[384,768]{1,0:T(8,128)(2,1)S(1)} %slice.7.piece_ref.refs_1_), channel_id=1, source_target_pairs={{0,8},{24,16},{1,9},{25,17},{2,10},{26,18},{3,11},{27,19},{4,12},{... | collective-permute-start | bytes 1769480 | tf_op jit(solution)/shard_map/ppermute | solution.py:282
  46.2 1.4 %collective-permute-start.3 = (bf16[384,640]{1,0:T(8,128)(2,1)}, bf16[384,640]{1,0:T(8,128)(2,1)}, u32[]{:S(2)}, u32[]{:S(2)}) collective-permute-start(bf16[384,640]{1,0:T(8,128)(2,1)} %given_part.3), channel_id=1, source_target_pairs={{8,16},{16,8},{9,17},{17,9},{10,18},{18,10},{11,19},{19,11},{12,20... | collective-permute-start | bytes 1474568 | tf_op jit(solution)/shard_map/ppermute | solution.py:285
  47.7 1.1 %slice.6.refs_2_.piece_ref = bf16[384,640]{1,0:T(8,128)(2,1)S(1)} slice(bf16[384,1408]{1,0:T(8,128)(2,1)} %bitcast.24), slice={[0:384], [768:1408]} | slice | bytes 983040 | tf_op jit(solution)/shard_map/slice | solution.py:281
  48.7 4.3 %all-to-all-start.2 = ((bf16[8,48,2048]{2,1,0:T(8,128)(2,1)}), bf16[8,48,2048]{2,1,0:T(8,128)(2,1)}, u32[]{:S(2)}, u32[]{:S(2)}) async-start(bf16[8,48,2048]{2,1,0:T(8,128)(2,1)} %bitcast.22), calls=%async_computation.2 | async-start | bytes 3145728 | tf_op jit(solution)/shard_map/all_to_all | solution.py:48
  53.1 3.3 %collective-permute-start.5 = (bf16[384,640]{1,0:T(8,128)(2,1)S(1)}, bf16[384,640]{1,0:T(8,128)(2,1)S(1)}, u32[]{:S(2)}, u32[]{:S(2)}) collective-permute-start(bf16[384,640]{1,0:T(8,128)(2,1)S(1)} %slice.6.refs_2_.piece_ref), channel_id=1, source_target_pairs={{0,8},{24,16},{1,9},{25,17},{2,10},{26,18},{3,11},{27,19},{4,12},{... | collective-permute-start | bytes 1474568 | tf_op jit(solution)/shard_map/ppermute | solution.py:282
  56.4 0.0 collective-permute-done.3.got_ref
  56.4 3.5 %collective-permute-done.2.piece_theirs_ref = bf16[384,768]{1,0:T(8,128)(2,1)S(1)} collective-permute-done((bf16[384,768]{1,0:T(8,128)(2,1)S(1)}, bf16[384,768]{1,0:T(8,128)(2,1)S(1)}, u32[]{:S(2)}, u32[]{:S(2)}) %collective-permute-start.2) | collective-permute-done | bytes 589856 | tf_op jit(solution)/shard_map/ppermute | solution.py:282
  59.9 1.4 %given_part.4 = bf16[384,768]{1,0:T(8,128)(2,1)S(1)} custom-call(s32[2]{0:T(128)S(1)} %add_convert_fusion.spot_ref, bf16[384,768]{1,0:T(8,128)(2,1)S(1)} %copy-done, bf16[384,768]{1,0:T(8,128)(2,1)S(1)} %collective-permute-done.theirs_ref, bf16[384,768]{1,0:T(8,128)(2,1)S(1)} %slice.7.piece_ref.refs_1_, ...), custom_call_target="tpu_custom_call" | custom-call | tf_op jit(solution)/shard_map/given_part/pallas_call | solution.py:20
  61.3 0.7 collective-permute-start.4
  62.0 0.0 copy-start.1
  62.0 1.9 %copy-done.1 = bf16[1,768,2048]{2,1,0:T(8,128)(2,1)S(1)} copy-done((bf16[1,768,2048]{2,1,0:T(8,128)(2,1)S(1)}, bf16[1,768,2048]{2,1,0:T(8,128)(2,1)}, u32[]{:S(2)}) %copy-start.1) | copy-done | bytes 3145752
  63.9 0.0 copy-start.3
  63.9 2.4 %grad_rows.1 = bf16[384,768]{1,0:T(8,128)(2,1)} custom-call(bf16[768,2048]{1,0:T(8,128)(2,1)S(1)} %bitcast.13, bf16[384,640]{1,0:T(8,128)(2,1)S(1)} %bitcast.16, bf16[384,768]{1,0:T(8,128)(2,1)S(1)} %slice.7.piece_ref.refs_1_, bf16[384,640]{1,0:T(8,128)(2,1)S(1)} %slice.6.refs_2_.piece_ref), custom_call_target="tpu_custom_call" | custom-call | tf_op jit(solution)/shard_map/grad_rows/pallas_call | solution.py:20
  66.3 0.0 copy-done.3
  66.3 1.3 %kept_part.3.keep_ref = bf16[384,640]{1,0:T(8,128)(2,1)S(1)} custom-call(s32[2]{0:T(128)S(1)} %add_convert_fusion.spot_ref, bf16[384,768]{1,0:T(8,128)(2,1)S(1)} %copy-done, bf16[384,768]{1,0:T(8,128)(2,1)S(1)} %collective-permute-done.theirs_ref, bf16[384,640]{1,0:T(8,128)(2,1)S(1)} %bitcast.17, bf16[384,640]{1,0:T(8,128)(2,1)S(1)} %copy-done.3), custom_call_target="tpu_custom_call" | custom-call | tf_op jit(solution)/shard_map/kept_part/pallas_call | solution.py:20
  67.6 1.6 %collective-permute-done.5.piece_theirs_ref = bf16[384,640]{1,0:T(8,128)(2,1)S(1)} collective-permute-done((bf16[384,640]{1,0:T(8,128)(2,1)S(1)}, bf16[384,640]{1,0:T(8,128)(2,1)S(1)}, u32[]{:S(2)}, u32[]{:S(2)}) %collective-permute-start.5) | collective-permute-done | bytes 491552 | tf_op jit(solution)/shard_map/ppermute | solution.py:282
  69.2 1.3 %given_part.5 = bf16[384,640]{1,0:T(8,128)(2,1)S(1)} custom-call(s32[2]{0:T(128)S(1)} %add_convert_fusion.spot_ref, bf16[384,768]{1,0:T(8,128)(2,1)S(1)} %copy-done, bf16[384,768]{1,0:T(8,128)(2,1)S(1)} %collective-permute-done.theirs_ref, bf16[384,640]{1,0:T(8,128)(2,1)S(1)} %slice.6.refs_2_.piece_ref, ...), custom_call_target="tpu_custom_call" | custom-call | tf_op jit(solution)/shard_map/given_part/pallas_call | solution.py:20
  70.5 0.7 collective-permute-start.6
  71.2 1.4 %kept_part.4.keep_ref = bf16[384,768]{1,0:T(8,128)(2,1)S(1)} custom-call(s32[2]{0:T(128)S(1)} %add_convert_fusion.spot_ref, bf16[384,768]{1,0:T(8,128)(2,1)S(1)} %copy-done, bf16[384,768]{1,0:T(8,128)(2,1)S(1)} %collective-permute-done.theirs_ref, bf16[384,768]{1,0:T(8,128)(2,1)S(1)} %slice.7.piece_ref.refs_1_, ...), custom_call_target="tpu_custom_call" | custom-call | tf_op jit(solution)/shard_map/kept_part/pallas_call | solution.py:20
  72.5 0.0 collective-permute-done.4.got_ref
  72.5 0.7 finish.4
  73.3 1.3 %collective-permute-start.8 = (bf16[192,768]{1,0:T(8,128)(2,1)S(1)}, bf16[192,768]{1,0:T(8,128)(2,1)S(1)}, u32[]{:S(2)}, u32[]{:S(2)}) collective-permute-start(bf16[192,768]{1,0:T(8,128)(2,1)S(1)} %get-tuple-element.45), channel_id=1, source_target_pairs={{8,0},{16,24},{9,1},{17,25},{10,2},{18,26},{11,3},{19,27},{12,4},{... | collective-permute-start | bytes 884744 | tf_op jit(solution)/shard_map/ppermute | solution.py:308
  74.6 1.3 %kept_part.5.keep_ref = bf16[384,640]{1,0:T(8,128)(2,1)S(1)} custom-call(s32[2]{0:T(128)S(1)} %add_convert_fusion.spot_ref, bf16[384,768]{1,0:T(8,128)(2,1)S(1)} %copy-done, bf16[384,768]{1,0:T(8,128)(2,1)S(1)} %collective-permute-done.theirs_ref, bf16[384,640]{1,0:T(8,128)(2,1)S(1)} %slice.6.refs_2_.piece_ref, ...), custom_call_target="tpu_custom_call" | custom-call | tf_op jit(solution)/shard_map/kept_part/pallas_call | solution.py:20
  75.9 0.0 copy-start.4
  75.9 0.0 copy-start.5
  75.9 1.2 %finish.3 = (bf16[192,640]{1,0:T(8,128)(2,1)S(1)}, bf16[192,640]{1,0:T(8,128)(2,1)S(1)}) custom-call(s32[2]{0:T(128)S(1)} %add_convert_fusion.spot_ref, bf16[384,640]{1,0:T(8,128)(2,1)S(1)} %kept_part.3.keep_ref, bf16[384,640]{1,0:T(8,128)(2,1)} %collective-permute-done.3.got_ref), custom_call_target="tpu_custom_call" | custom-call | tf_op jit(solution)/shard_map/finish/pallas_call | solution.py:20
  77.1 0.0 collective-permute-done.6.got_ref
  77.1 0.7 finish.5
  77.8 1.3 %collective-permute-start.9 = (bf16[192,640]{1,0:T(8,128)(2,1)S(1)}, bf16[192,640]{1,0:T(8,128)(2,1)S(1)}, u32[]{:S(2)}, u32[]{:S(2)}) collective-permute-start(bf16[192,640]{1,0:T(8,128)(2,1)S(1)} %get-tuple-element.46), channel_id=1, source_target_pairs={{8,0},{16,24},{9,1},{17,25},{10,2},{18,26},{11,3},{19,27},{12,4},{... | collective-permute-start | bytes 737288 | tf_op jit(solution)/shard_map/ppermute | solution.py:308
  79.1 1.3 %collective-permute-start.7 = (bf16[192,640]{1,0:T(8,128)(2,1)S(1)}, bf16[192,640]{1,0:T(8,128)(2,1)S(1)}, u32[]{:S(2)}, u32[]{:S(2)}) collective-permute-start(bf16[192,640]{1,0:T(8,128)(2,1)S(1)} %get-tuple-element.44), channel_id=1, source_target_pairs={{8,0},{16,24},{9,1},{17,25},{10,2},{18,26},{11,3},{19,27},{12,4},{... | collective-permute-start | bytes 737288 | tf_op jit(solution)/shard_map/ppermute | solution.py:308
  80.4 0.0 all-to-all-done.2
  80.4 0.0 copy-done.4
  80.4 0.0 copy-done.5
  80.5 3.1 %combine.1 = bf16[128,2048]{1,0:T(8,128)(2,1)} custom-call(s32[2,128]{1,0:T(2,128)S(1)} %bitcast.19, f32[2,128]{1,0:T(2,128)S(1)} %bitcast.21, bf16[384,2048]{1,0:T(8,128)(2,1)} %bitcast.10.returned_ref), custom_call_target="tpu_custom_call" | custom-call | tf_op jit(solution)/shard_map/combine/pallas_call | solution.py:20
  83.6 14.2 %collective-permute-done.9.refs_5_ = bf16[192,640]{1,0:T(8,128)(2,1)S(1)} collective-permute-done((bf16[192,640]{1,0:T(8,128)(2,1)S(1)}, bf16[192,640]{1,0:T(8,128)(2,1)S(1)}, u32[]{:S(2)}, u32[]{:S(2)}) %collective-permute-start.9) | collective-permute-done | bytes 245792 | tf_op jit(solution)/shard_map/ppermute | solution.py:308
  97.8 2.6 %collective-permute-done.7.refs_3_ = bf16[192,640]{1,0:T(8,128)(2,1)S(1)} collective-permute-done((bf16[192,640]{1,0:T(8,128)(2,1)S(1)}, bf16[192,640]{1,0:T(8,128)(2,1)S(1)}, u32[]{:S(2)}, u32[]{:S(2)}) %collective-permute-start.7) | collective-permute-done | bytes 245792 | tf_op jit(solution)/shard_map/ppermute | solution.py:308
  100.5 0.0 collective-permute-done.8.refs_4_
  100.5 1.5 %shares.1 = bf16[192,2048]{1,0:T(8,128)(2,1)} custom-call(s32[2]{0:T(128)S(1)} %add_convert_fusion.spot_ref, bf16[192,640]{1,0:T(8,128)(2,1)S(1)} %get-tuple-element.36.refs_0_, bf16[192,768]{1,0:T(8,128)(2,1)S(1)} %get-tuple-element.39.refs_1_, bf16[192,640]{1,0:T(8,128)(2,1)S(1)} %get-tuple-element.43.refs_2_, ...), custom_call_target="tpu_custom_call" | custom-call | tf_op jit(solution)/shard_map/shares/pallas_call | solution.py:20
Async XLA Ops:
  0.6 17.8 %collective-permute-start = (bf16[384,768]{1,0:T(8,128)(2,1)}, bf16[384,768]{1,0:T(8,128)(2,1)S(1)}, u32[]{:S(2)}, u32[]{:S(2)}) collective-permute-start(bf16[384,768]{1,0:T(8,128)(2,1)} %mine_ref.11), channel_id=1, source_target_pairs={{0,8},{24,16},{1,9},{25,17},{2,10},{26,18},{3,11},{27,19},{4,12},{... | collective-permute-start | bytes 1769480 | tf_op jit(solution)/shard_map/ppermute | solution.py:257
  8.3 12.2 %all-to-all-start.1 = ((bf16[8,48,640]{2,1,0:T(8,128)(2,1)}), bf16[8,48,640]{2,1,0:T(8,128)(2,1)S(1)}, u32[]{:S(2)}, u32[]{:S(2)}) async-start(bf16[8,48,640]{2,1,0:T(8,128)(2,1)} %bitcast.27), calls=%async_computation.1 | async-start | bytes 983040 | tf_op jit(solution)/shard_map/all_to_all | solution.py:48
  16.3 21.3 %copy-start = (bf16[384,768]{1,0:T(8,128)(2,1)S(1)}, bf16[384,768]{1,0:T(8,128)(2,1)}, u32[]{:S(2)}) copy-start(bf16[384,768]{1,0:T(8,128)(2,1)} %mine_ref.11) | copy-start | bytes 1769476
  20.5 19.2 %all-to-all-start = ((bf16[8,48,1408]{2,1,0:T(8,128)(2,1)}), bf16[8,48,1408]{2,1,0:T(8,128)(2,1)S(1)}, u32[]{:S(2)}, u32[]{:S(2)}) async-start(bf16[8,48,1408]{2,1,0:T(8,128)(2,1)} %bitcast.25), calls=%async_computation | async-start | bytes 2162688 | tf_op jit(solution)/shard_map/all_to_all | solution.py:48
  24.1 13.5 %collective-permute-start.1 = (bf16[384,640]{1,0:T(8,128)(2,1)S(1)}, bf16[384,640]{1,0:T(8,128)(2,1)S(1)}, u32[]{:S(2)}, u32[]{:S(2)}) collective-permute-start(bf16[384,640]{1,0:T(8,128)(2,1)S(1)} %bitcast.14), channel_id=1, source_target_pairs={{0,8},{24,16},{1,9},{25,17},{2,10},{26,18},{3,11},{27,19},{4,12},{... | collective-permute-start | bytes 1474568 | tf_op jit(solution)/shard_map/ppermute | solution.py:275
  37.6 2.1 %copy-start.2 = (bf16[384,640]{1,0:T(8,128)(2,1)}, bf16[384,640]{1,0:T(8,128)(2,1)S(1)}, u32[]{:S(2)}) copy-start(bf16[384,640]{1,0:T(8,128)(2,1)S(1)} %collective-permute-done.1.piece_theirs_ref) | copy-start | bytes 1474564
  39.7 1.0 copy-start.6
  41.8 18.1 %collective-permute-start.2 = (bf16[384,768]{1,0:T(8,128)(2,1)S(1)}, bf16[384,768]{1,0:T(8,128)(2,1)S(1)}, u32[]{:S(2)}, u32[]{:S(2)}) collective-permute-start(bf16[384,768]{1,0:T(8,128)(2,1)S(1)} %slice.7.piece_ref.refs_1_), channel_id=1, source_target_pairs={{0,8},{24,16},{1,9},{25,17},{2,10},{26,18},{3,11},{27,19},{4,12},{... | collective-permute-start | bytes 1769480 | tf_op jit(solution)/shard_map/ppermute | solution.py:282
  46.2 10.2 %collective-permute-start.3 = (bf16[384,640]{1,0:T(8,128)(2,1)}, bf16[384,640]{1,0:T(8,128)(2,1)}, u32[]{:S(2)}, u32[]{:S(2)}) collective-permute-start(bf16[384,640]{1,0:T(8,128)(2,1)} %given_part.3), channel_id=1, source_target_pairs={{8,16},{16,8},{9,17},{17,9},{10,18},{18,10},{11,19},{19,11},{12,20... | collective-permute-start | bytes 1474568 | tf_op jit(solution)/shard_map/ppermute | solution.py:285
  48.7 31.7 %all-to-all-start.2 = ((bf16[8,48,2048]{2,1,0:T(8,128)(2,1)}), bf16[8,48,2048]{2,1,0:T(8,128)(2,1)}, u32[]{:S(2)}, u32[]{:S(2)}) async-start(bf16[8,48,2048]{2,1,0:T(8,128)(2,1)} %bitcast.22), calls=%async_computation.2 | async-start | bytes 3145728 | tf_op jit(solution)/shard_map/all_to_all | solution.py:48
  53.1 16.1 %collective-permute-start.5 = (bf16[384,640]{1,0:T(8,128)(2,1)S(1)}, bf16[384,640]{1,0:T(8,128)(2,1)S(1)}, u32[]{:S(2)}, u32[]{:S(2)}) collective-permute-start(bf16[384,640]{1,0:T(8,128)(2,1)S(1)} %slice.6.refs_2_.piece_ref), channel_id=1, source_target_pairs={{0,8},{24,16},{1,9},{25,17},{2,10},{26,18},{3,11},{27,19},{4,12},{... | collective-permute-start | bytes 1474568 | tf_op jit(solution)/shard_map/ppermute | solution.py:282
  61.3 11.3 %collective-permute-start.4 = (bf16[384,768]{1,0:T(8,128)(2,1)S(1)}, bf16[384,768]{1,0:T(8,128)(2,1)S(1)}, u32[]{:S(2)}, u32[]{:S(2)}) collective-permute-start(bf16[384,768]{1,0:T(8,128)(2,1)S(1)} %given_part.4), channel_id=1, source_target_pairs={{8,16},{16,8},{9,17},{17,9},{10,18},{18,10},{11,19},{19,11},{12,20... | collective-permute-start | bytes 1769480 | tf_op jit(solution)/shard_map/ppermute | solution.py:291
  62.0 1.9 %copy-start.1 = (bf16[1,768,2048]{2,1,0:T(8,128)(2,1)S(1)}, bf16[1,768,2048]{2,1,0:T(8,128)(2,1)}, u32[]{:S(2)}) copy-start(bf16[1,768,2048]{2,1,0:T(8,128)(2,1)} %param.9) | copy-start | bytes 9437188
  63.9 2.4 %copy-start.3 = (bf16[384,640]{1,0:T(8,128)(2,1)S(1)}, bf16[384,640]{1,0:T(8,128)(2,1)}, u32[]{:S(2)}) copy-start(bf16[384,640]{1,0:T(8,128)(2,1)} %copy-done.2) | copy-start | bytes 1474564
  70.5 6.6 %collective-permute-start.6 = (bf16[384,640]{1,0:T(8,128)(2,1)S(1)}, bf16[384,640]{1,0:T(8,128)(2,1)S(1)}, u32[]{:S(2)}, u32[]{:S(2)}) collective-permute-start(bf16[384,640]{1,0:T(8,128)(2,1)S(1)} %given_part.5), channel_id=1, source_target_pairs={{8,16},{16,8},{9,17},{17,9},{10,18},{18,10},{11,19},{19,11},{12,20... | collective-permute-start | bytes 1474568 | tf_op jit(solution)/shard_map/ppermute | solution.py:299
  73.3 27.2 %collective-permute-start.8 = (bf16[192,768]{1,0:T(8,128)(2,1)S(1)}, bf16[192,768]{1,0:T(8,128)(2,1)S(1)}, u32[]{:S(2)}, u32[]{:S(2)}) collective-permute-start(bf16[192,768]{1,0:T(8,128)(2,1)S(1)} %get-tuple-element.45), channel_id=1, source_target_pairs={{8,0},{16,24},{9,1},{17,25},{10,2},{18,26},{11,3},{19,27},{12,4},{... | collective-permute-start | bytes 884744 | tf_op jit(solution)/shard_map/ppermute | solution.py:308
  75.9 4.6 %copy-start.4 = (s32[128,2]{0,1:T(2,128)S(1)}, s32[128,2]{0,1:T(2,128)}, u32[]{:S(2)}) copy-start(s32[128,2]{0,1:T(2,128)} %param.7) | copy-start | bytes 3076
  75.9 4.6 %copy-start.5 = (f32[128,2]{0,1:T(2,128)S(1)}, f32[128,2]{0,1:T(2,128)}, u32[]{:S(2)}) copy-start(f32[128,2]{0,1:T(2,128)} %param.8) | copy-start | bytes 3076
  77.8 20.0 %collective-permute-start.9 = (bf16[192,640]{1,0:T(8,128)(2,1)S(1)}, bf16[192,640]{1,0:T(8,128)(2,1)S(1)}, u32[]{:S(2)}, u32[]{:S(2)}) collective-permute-start(bf16[192,640]{1,0:T(8,128)(2,1)S(1)} %get-tuple-element.46), channel_id=1, source_target_pairs={{8,0},{16,24},{9,1},{17,25},{10,2},{18,26},{11,3},{19,27},{12,4},{... | collective-permute-start | bytes 737288 | tf_op jit(solution)/shard_map/ppermute | solution.py:308
  79.1 21.3 %collective-permute-start.7 = (bf16[192,640]{1,0:T(8,128)(2,1)S(1)}, bf16[192,640]{1,0:T(8,128)(2,1)S(1)}, u32[]{:S(2)}, u32[]{:S(2)}) collective-permute-start(bf16[192,640]{1,0:T(8,128)(2,1)S(1)} %get-tuple-element.44), channel_id=1, source_target_pairs={{8,0},{16,24},{9,1},{17,25},{10,2},{18,26},{11,3},{19,27},{12,4},{... | collective-permute-start | bytes 737288 | tf_op jit(solution)/shard_map/ppermute | solution.py:308
